TPU v7x, 256 devices: a whole 4x4x8 slice. The times are simulated.
256 devices in a mesh: front: 16 (over z, y_hi), row: 8 (over x, core), col: 2 (over y_lo).
Axes of the slice: x: 4, y: 4 (y_hi: 2, y_lo: 2; y = y_hi * 2 + y_lo), z: 8, core: 2. Of those that a mesh axis runs over, the one named last changes fastest.
Arguments:
- update_block: float32 [16, 4096, 4096], P('front', 'row', 'col'), may hold values from -6 to 6
- front_panel: float32 [16, 4096, 768], P('front', 'row', 'col'), may hold values from -6 to 6
- inverse_factor: float32 [16, 768, 768], P('front', None, 'col'), as said below
- child_tiles: bfloat16 [22016, 128, 128], P(('front', 'row', 'col')), may hold values from -6 to 6
- child_target: int32 [22016, 1], P(('front', 'row', 'col')), may hold values from 0 to 127; in each aligned block of 86 rows (0 to 85, 86 to 171, ...) at most 2 rows name the same one
- child_row: int32 [22016], P(('front', 'row', 'col')), may hold values from 0 to 3
- child_col: int32 [22016], P(('front', 'row', 'col')), may hold values from 0 to 15
- front_owner: int32 [16], replicated, may hold values from 0 to 15, each once
- live_tiles: int32 [16], P('front'), may hold values from 16 to 32
Outputs:
- schur: bfloat16 [16, 4096, 4096], P('front', 'row', 'col')
- panel: float32 [16, 4096, 768], P('front', 'row', 'col')
Inputs may be any that keep to these rules, and one draw needn't show every extreme that they name: `inverse_factor`: lower triangular with a positive diagonal. `child_target`: in the rows of one device no value appears more than 2 times, and some value appears exactly 2 times. `front_owner`: each slot holds one front.
All inputs are finite; a program needn't handle non-finite values.
Results may differ from a plain program's by a relative error of at most 0.001.
Values may be sent and summed in bfloat16 or wider, within the bound.
A program may use at most 128 MiB of HBM per device.

v0:
```python
import jax
import jax.numpy as jnp
from jax import lax
from jax.sharding import PartitionSpec as P

TILE = 128
CAP = 2


def per_device(
    update_block,
    front_panel,
    inverse_factor,
    child_tiles,
    child_target,
    child_row,
    child_col,
    front_owner,
    live_tiles,
):
    highest = lax.Precision.HIGHEST
    rows_dev = update_block.shape[1]
    cols_dev = update_block.shape[2]
    front_count = lax.axis_size("front")
    row_count = lax.axis_size("row")
    col_count = lax.axis_size("col")
    row_place = lax.axis_index("row")
    col_place = lax.axis_index("col")
    live_bound = live_tiles[0] * TILE
    row_ids = row_place * rows_dev + jnp.arange(rows_dev, dtype=jnp.int32)
    col_ids = col_place * cols_dev + jnp.arange(cols_dev, dtype=jnp.int32)
    partial_value = lax.dot_general(
        front_panel[0],
        inverse_factor[0],
        (((1,), (1,)), ((), ())),
        precision=highest,
        preferred_element_type=jnp.float32,
    )
    partial_value = jnp.where(
        row_ids[:, None] < live_bound, partial_value, jnp.zeros_like(partial_value)
    )
    own_panel = lax.psum(partial_value, "col")
    full_panel = lax.all_gather(own_panel, "row", axis=0, tiled=True)
    columns = lax.dynamic_slice_in_dim(full_panel, col_place * cols_dev, cols_dev, 0)
    half_width = inverse_factor.shape[1] // col_count
    panel_out = lax.dynamic_slice_in_dim(own_panel, col_place * half_width, half_width, 1)[None]
    dest_count = front_count * row_count
    targets = child_target[:, 0]
    fronts = jnp.arange(front_owner.shape[0], dtype=jnp.int32)
    holder = jnp.sum(
        jnp.where((targets // row_count)[:, None] == fronts[None, :], front_owner[None, :], 0),
        axis=1,
    )
    address = holder * row_count + targets % row_count
    flagged = (address[:, None] == jnp.arange(dest_count, dtype=jnp.int32)[None, :]).astype(
        jnp.int32
    )
    earlier = jnp.cumsum(flagged, axis=0) - flagged
    within = jnp.sum(earlier * flagged, axis=1)
    position = address * CAP + within
    row_tiles = rows_dev // TILE
    col_tiles = cols_dev // TILE
    tile_count = row_tiles * col_tiles
    places = child_row * col_tiles + child_col
    outgoing = jnp.zeros((dest_count * CAP, TILE, TILE), jnp.bfloat16).at[position].set(child_tiles)
    labels = jnp.full((dest_count * CAP,), tile_count, jnp.int32).at[position].set(places)
    incoming, in_labels = (
        lax.all_to_all(
            outgoing.reshape(dest_count, CAP, TILE, TILE),
            ("front", "row"),
            split_axis=0,
            concat_axis=0,
            tiled=True,
        ),
        lax.all_to_all(
            labels.reshape(dest_count, CAP),
            ("front", "row"),
            split_axis=0,
            concat_axis=0,
            tiled=True,
        ),
    )
    flat_tiles = incoming.reshape(dest_count * CAP, TILE * TILE)
    tile_tags = in_labels.reshape(dest_count * CAP)
    selector = (jnp.arange(tile_count, dtype=jnp.int32)[:, None] == tile_tags[None, :]).astype(
        jnp.bfloat16
    )
    assembled = jnp.dot(selector, flat_tiles, preferred_element_type=jnp.float32)
    assembled = (
        assembled.reshape(row_tiles, col_tiles, TILE, TILE)
        .transpose(0, 2, 1, 3)
        .reshape(rows_dev, cols_dev)
    )
    outer_part = lax.dot_general(
        own_panel,
        columns,
        (((1,), (1,)), ((), ())),
        precision=highest,
        preferred_element_type=jnp.float32,
    )
    updated = update_block[0] + assembled - outer_part
    inside = (row_ids[:, None] < live_bound) & (col_ids[None, :] < live_bound)
    schur_out = jnp.where(inside, updated, jnp.zeros_like(updated)).astype(jnp.bfloat16)[None]
    return (schur_out, panel_out)


def solution(mesh):
    return jax.shard_map(
        per_device,
        mesh=mesh,
        in_specs=(
            P("front", "row", "col"),
            P("front", "row", "col"),
            P("front", None, "col"),
            P(("front", "row", "col"), None, None),
            P(("front", "row", "col"), None),
            P(("front", "row", "col")),
            P(("front", "row", "col")),
            P(),
            P("front"),
        ),
        out_specs=(P("front", "row", "col"), P("front", "row", "col")),
        check_vma=False,
    )
```

profile of v0, /device:TPU:1, one launch (start us, length us, event | category | flops | bytes accessed | tf_op | source)
XLA Modules:
  0.0 384.8 jit_solution(16489483978283424103)
XLA Ops:
  7.2 0.0 all-reduce.2.cloned.1.call-start
  8.0 0.4 copy-done
  8.5 5.0 %convolution_select_fusion = f32[512,768]{1,0:T(8,128)} fusion(f32[1,768,384]{2,1,0:T(8,128)S(1)} %copy-done, f32[1,512,384]{2,1,0:T(8,128)} %param.10, pred[512]{0:T(512)(128)(4,1)S(1)} %add_compare_fusion.1), kind=kOutput, calls=%fused_computation.10 | convolution fusion | flops 1812332544 | bytes 3539456 | tf_op jit(solution)/shard_map/dot_general | solution.py:32
  13.5 0.0 all-gather.2.cloned.1.call-start
  13.5 67.1 %all-reduce.2.cloned.1.call-done = f32[512,768]{1,0:T(8,128)} async-done(((f32[512,768]{1,0:T(8,128)}), f32[512,768]{1,0:T(8,128)}) %all-reduce.2.cloned.1.call-update) | async-done | bytes 1572880 | tf_op jit(solution)/shard_map/psum | solution.py:42
  80.7 0.1 select_reduce_fusion.1
  80.8 0.1 fusion.15
  80.9 0.1 reduce_window_sum.11
  81.0 0.2 select_reduce_fusion
  81.2 0.8 scatter_custom_fusion
  82.1 0.8 all_to_all.9
  82.9 13.6 %all-to-all-start = ((s32[128,1,2]{2,1,0:T(1,128)}), s32[128,1,2]{2,1,0:T(1,128)S(1)}, u32[]{:S(2)}, u32[]{:S(2)}) async-start(s32[128,1,2]{2,1,0:T(1,128)} %bitcast.7), calls=%async_computation | async-start | bytes 131072 | tf_op jit(solution)/shard_map/all_to_all | solution.py:75
  96.5 5.5 %broadcast_in_dim.52 = bf16[256,128,128]{2,1,0:T(8,128)(2,1)} broadcast(bf16[]{:T(256)} %constant.65.clone.1), dimensions={} | broadcast | bytes 8388610 | tf_op jit(solution)/shard_map/broadcast_in_dim | solution.py:65
  102.0 14.6 %scatter_fusion = bf16[256,128,128]{2,1,0:T(8,128)(2,1)} fusion(bf16[256,128,128]{2,1,0:T(8,128)(2,1)} %broadcast_in_dim.52, s32[86]{0:T(128)S(1)} %fusion.19, bf16[86,128,128]{2,1,0:T(8,128)(2,1)} %param.12), kind=kCustom, calls=%fused_computation.1 | custom fusion | bytes 8454488 | tf_op jit(solution)/shard_map/scatter | solution.py:65
  116.6 14.6 %all-to-all-start.1 = ((bf16[128,2,128,128]{3,2,1,0:T(8,128)(2,1)}), bf16[128,2,128,128]{3,2,1,0:T(8,128)(2,1)}, u32[]{:S(2)}, u32[]{:S(2)}) async-start(bf16[128,2,128,128]{3,2,1,0:T(8,128)(2,1)} %bitcast.59), calls=%async_computation.1 | async-start | bytes 16777216 | tf_op jit(solution)/shard_map/all_to_all | solution.py:68
  131.2 0.5 broadcast.104
  131.8 0.8 reduce.3
  132.6 0.1 eq.70
  132.7 0.9 dynamic-slice_bitcast_fusion
  133.7 185.9 %all-to-all-done.1 = bf16[128,2,128,128]{3,2,1,0:T(8,128)(2,1)} async-done(((bf16[128,2,128,128]{3,2,1,0:T(8,128)(2,1)}), bf16[128,2,128,128]{3,2,1,0:T(8,128)(2,1)}, u32[]{:S(2)}, u32[]{:S(2)}) %all-to-all-start.1) | async-done | bytes 8388640 | tf_op jit(solution)/shard_map/all_to_all | solution.py:68
  319.6 23.2 %copy.23 = bf16[32,8,128,128]{3,1,2,0:T(8,128)(2,1)} copy(bf16[32,8,128,128]{3,2,1,0:T(8,128)(2,1)} %bitcast.22) | data formatting | bytes 16777216
  342.8 11.9 %copy.15 = bf16[16384,256]{1,0:T(8,128)(2,1)} copy(bf16[16384,256]{0,1:T(8,128)(2,1)} %bitcast.60) | data formatting | bytes 16777216 | tf_op jit(solution)/shard_map/dot_general | solution.py:88
  354.7 8.0 %fusion.12 = f32[4,16,128,128]{3,1,2,0:T(8,128)} fusion(bf16[128,128,256,1]{2,1,0,3:T(8,128)(2,1)} %bitcast.62, s32[256]{0:T(256)S(1)} %eq.70, s32[4,16]{1,0:T(4,128)S(1)} %multiply_add_fusion), kind=kOutput, calls=%fused_computation.14 | convolution fusion | flops 536887296 | bytes 12584192 | tf_op jit(solution)/shard_map/dot_general | solution.py:88
  362.7 15.3 %fusion.7 = bf16[1,512,2048]{2,1,0:T(8,128)(2,1)} fusion(f32[512,768]{1,0:T(8,128)S(1)} %copy-done.1, f32[4096,768]{1,0:T(8,128)} %all-gather.2.cloned.1.call-done, s32[]{:T(128)S(6)} %select_n.43, f32[64,8,16,128]{3,2,1,0:T(8,128)} %bitcast.61, f32[1,512,2048]{2,1,0:T(8,128)} %param.9, pred[2048]{0:T(1024)(128)(4,1)S(1)} %add_compare_fusion, ...), kind=kOutput, calls=%fused_computation.9 | convolution fusion | flops 9668919296 | bytes 18352644 | tf_op jit(solution)/shard_map/dot_general | solution.py:94
  (22 shorter events, 0.1 us)
Async XLA Ops:
  7.2 1.3 copy-start
  7.2 73.5 %copy-start.3 = (s32[86,1]{0,1:T(1,128)S(1)}, s32[86,1]{0,1:T(1,128)}, u32[]{:S(2)}) copy-start(s32[86,1]{0,1:T(1,128)} %param.13) | copy-start | bytes 1036
  7.2 73.5 %copy-start.2 = (s32[16]{0:T(128)S(1)}, s32[16]{0:T(128)}, u32[]{:S(2)}) copy-start(s32[16]{0:T(128)} %param.16) | copy-start | bytes 196
  7.2 74.0 %copy-start.5 = (s32[86]{0:T(128)S(1)}, s32[86]{0:T(128)}, u32[]{:S(2)}) copy-start(s32[86]{0:T(128)} %param.14) | copy-start | bytes 1036
  7.2 74.0 %copy-start.4 = (s32[86]{0:T(128)S(1)}, s32[86]{0:T(128)}, u32[]{:S(2)}) copy-start(s32[86]{0:T(128)} %param.15) | copy-start | bytes 1036
  7.2 73.4 %all-reduce.2.cloned.1.call-start = ((), (), s32[]{:S(2)}) async-start(), calls=%async_computation.2 | async-start | bytes 3145728 | tf_op jit(solution)/shard_map/psum | solution.py:42
  13.5 349.3 %all-gather.2.cloned.1.call-start = ((), (), s32[]{:S(2)}) async-start(), calls=%async_computation.3 | async-start | bytes 14155776 | tf_op jit(solution)/shard_map/all_gather | solution.py:43
  82.9 33.8 %all-to-all-start = ((s32[128,1,2]{2,1,0:T(1,128)}), s32[128,1,2]{2,1,0:T(1,128)S(1)}, u32[]{:S(2)}, u32[]{:S(2)}) async-start(s32[128,1,2]{2,1,0:T(1,128)} %bitcast.7), calls=%async_computation | async-start | bytes 131072 | tf_op jit(solution)/shard_map/all_to_all | solution.py:75
  116.6 16.1 %copy-start.1 = (f32[512,768]{1,0:T(8,128)S(1)}, f32[512,768]{1,0:T(8,128)}, u32[]{:S(2)}) copy-start(f32[512,768]{1,0:T(8,128)} %all-reduce.2.cloned.1.call-done) | copy-start | bytes 4718596
  116.6 202.9 %all-to-all-start.1 = ((bf16[128,2,128,128]{3,2,1,0:T(8,128)(2,1)}), bf16[128,2,128,128]{3,2,1,0:T(8,128)(2,1)}, u32[]{:S(2)}, u32[]{:S(2)}) async-start(bf16[128,2,128,128]{3,2,1,0:T(8,128)(2,1)} %bitcast.59), calls=%async_computation.1 | async-start | bytes 16777216 | tf_op jit(solution)/shard_map/all_to_all | solution.py:68
Sparse Core Ops, SparseCore 0:
  13.6 67.0 all-reduce.1
  82.6 103.4 all-gather.1
where the time goes:
time: 386 us; the launch traced here: 385 us
  waiting for transfers between devices  253 us (66%)
  local copies, waits for them, and re-layouts  59 us (15%)
  starting transfers between devices  28.2 us (7%)
  matrix products  28.2 us (7%)
  between operations  14.9 us (4%)
    all_to_all x1, waiting for transfers between devices, per_device(): lax.all_to_all(outgoing.reshape(dest_count, CAP, TILE, TILE), ('front', '...  186 us
    psum x1, waiting for transfers between devices, per_device(): own_panel = lax.psum(partial_value, 'col')  67.1 us
    unnamed x13, local copies, waits for them, and re-layouts  23.7 us
    dot_general x1, matrix products, per_device(): lax.dot_general(own_panel, columns, (((1,), (1,)), ((), ())), precision=h...  15.3 us
    scatter x1, local copies, waits for them, and re-layouts, per_device(): jnp.zeros((dest_count * CAP, TILE, TILE), jnp.bfloat16).at[position]  14.6 us
    all_to_all x1, starting transfers between devices, per_device(): lax.all_to_all(outgoing.reshape(dest_count, CAP, TILE, TILE), ('front', '...  14.6 us
    all_to_all x1, starting transfers between devices, per_device(): lax.all_to_all(labels.reshape(dest_count, CAP), ('front', 'row'), split_a...  13.6 us
    dot_general x1, local copies, waits for them, and re-layouts, per_device(): jnp.dot(selector, flat_tiles, preferred_element_type=jnp.float32)  11.9 us
  transfers between devices with their start and end apart: 4, of which 2 were waited for; matrix products, arithmetic and copies ran while one was open for 17% of the time, Pallas kernels for 0%

commit v1 on v0

v1 whole, which is shorter than its diff:
```python
import functools

import jax
import jax.numpy as jnp
from jax import lax
from jax.experimental import pallas as pl
from jax.experimental.pallas import tpu as pltpu
from jax.sharding import PartitionSpec as P

TILE = 128
CAP = 2
MESH = pl.DeviceIdType.MESH


def pack_kernel(dests, rows_n, col_tiles, target, crow, ccol, owner, tiles, out, lab, count, sem):
    amount = tiles.shape[0]
    empty = 4 * col_tiles
    lab[...] = jnp.full(lab.shape, empty, jnp.int32)

    @pl.loop(0, dests)
    def _(i):
        count[i] = 0

    lane = lax.broadcasted_iota(jnp.int32, (1, 128), 1)

    @pl.loop(0, amount)
    def _(i):
        t = target[i]
        address = owner[t // rows_n] * rows_n + t % rows_n
        k = count[address]
        count[address] = k + 1
        pltpu.make_async_copy(tiles.at[i], out.at[k * dests + address], sem).start()
        place = crow[i] * col_tiles + ccol[i]
        lab[address] = jnp.where(lane == k, place, lab[address])

    pltpu.make_async_copy(tiles, out.at[pl.ds(0, amount)], sem).wait()


def peer_of(step, me, dests):
    return jnp.bitwise_xor(me, (step * 37) % dests)


def exchange_kernel(dests, rows_n, slot, with_lab, *refs):
    if with_lab:
        out, lab, inc, inclab, ssem, rsem, lsem, lssem, lrsem = refs
    else:
        out, inc, ssem, rsem, lsem = refs
    me = lax.axis_index("front") * rows_n + lax.axis_index("row")
    col = lax.axis_index("col")

    own = pltpu.make_async_copy(out.at[slot * dests + me], inc.at[me], lsem.at[0])
    own.start()
    if with_lab:
        ownlab = pltpu.make_async_copy(lab.at[me], inclab.at[me], lsem.at[1])
        ownlab.start()

    @pl.loop(1, dests)
    def _(step):
        p = peer_of(step, me, dests)
        dev = (p // rows_n, p % rows_n, col)
        pltpu.make_async_remote_copy(
            out.at[slot * dests + p], inc.at[me], ssem, rsem, device_id=dev, device_id_type=MESH
        ).start()
        if with_lab:
            pltpu.make_async_remote_copy(
                lab.at[p], inclab.at[me], lssem, lrsem, device_id=dev, device_id_type=MESH
            ).start()

    own.wait()
    some = pl.ds(0, dests - 1)
    both = pltpu.make_async_remote_copy(
        out.at[some], inc.at[some], ssem, rsem, device_id=(0, 0, 0), device_id_type=MESH
    )
    both.wait_send()
    both.wait_recv()
    if with_lab:
        ownlab.wait()
        labs = pltpu.make_async_remote_copy(
            lab.at[some], inclab.at[some], lssem, lrsem, device_id=(0, 0, 0), device_id_type=MESH
        )
        labs.wait_send()
        labs.wait_recv()


def assemble_kernel(group, col_tiles, lab, update, first, second, out):
    step = pl.program_id(0)
    empty = 4 * col_tiles

    @pl.when(step == 0)
    def _():
        out[...] = update[...]

    def add(place, tile):
        @pl.when(place < empty)
        def _():
            r = pl.multiple_of((place // col_tiles) * TILE, TILE)
            c = pl.multiple_of((place % col_tiles) * TILE, TILE)
            out[pl.ds(r, TILE), pl.ds(c, TILE)] += tile[...].astype(jnp.float32)

    @pl.loop(0, group)
    def _(j):
        add(lab[step * group + j, 0, 0], first.at[j])
        add(lab[step * group + j, 0, 1], second.at[j])


def per_device(
    update_block,
    front_panel,
    inverse_factor,
    child_tiles,
    child_target,
    child_row,
    child_col,
    front_owner,
    live_tiles,
):
    highest = lax.Precision.HIGHEST
    rows_dev = update_block.shape[1]
    cols_dev = update_block.shape[2]
    front_count = lax.axis_size("front")
    row_count = lax.axis_size("row")
    col_count = lax.axis_size("col")
    row_place = lax.axis_index("row")
    col_place = lax.axis_index("col")
    live_bound = live_tiles[0] * TILE
    row_ids = row_place * rows_dev + jnp.arange(rows_dev, dtype=jnp.int32)
    col_ids = col_place * cols_dev + jnp.arange(cols_dev, dtype=jnp.int32)
    dests = front_count * row_count
    col_tiles = cols_dev // TILE

    anyspace = pl.BlockSpec(memory_space=pl.ANY)
    smem = pl.BlockSpec(memory_space=pltpu.SMEM)
    tile_shape = (TILE, TILE)
    outgoing, labels = pl.pallas_call(
        functools.partial(pack_kernel, dests, row_count, col_tiles),
        out_shape=(
            jax.ShapeDtypeStruct((CAP * dests,) + tile_shape, jnp.bfloat16),
            jax.ShapeDtypeStruct((dests, 1, 128), jnp.int32),
        ),
        in_specs=[smem, smem, smem, smem, anyspace],
        out_specs=(anyspace, pl.BlockSpec(memory_space=pltpu.VMEM)),
        scratch_shapes=[pltpu.SMEM((dests,), jnp.int32), pltpu.SemaphoreType.DMA],
        name="pack",
    )(child_target[:, 0], child_row, child_col, front_owner, child_tiles)

    partial_value = lax.dot_general(
        front_panel[0],
        inverse_factor[0],
        (((1,), (1,)), ((), ())),
        precision=highest,
        preferred_element_type=jnp.float32,
    )
    partial_value = jnp.where(
        row_ids[:, None] < live_bound, partial_value, jnp.zeros_like(partial_value)
    )
    own_panel = lax.psum(partial_value, "col")

    inc_shape = jax.ShapeDtypeStruct((dests,) + tile_shape, jnp.bfloat16)
    dma = pltpu.SemaphoreType.DMA
    cost = pl.CostEstimate(flops=0, bytes_accessed=300_000_000, transcendentals=0)
    first, in_labels = pl.pallas_call(
        functools.partial(exchange_kernel, dests, row_count, 0, True),
        out_shape=(inc_shape, jax.ShapeDtypeStruct((dests, 1, 128), jnp.int32)),
        in_specs=[anyspace, anyspace],
        out_specs=(anyspace, anyspace),
        scratch_shapes=[dma, dma, dma((2,)), dma, dma],
        compiler_params=pltpu.CompilerParams(has_side_effects=True),
        cost_estimate=cost,
        name="exchange_a",
    )(outgoing, labels)
    outgoing, own_panel, first = lax.optimization_barrier((outgoing, own_panel, first))
    full_panel = lax.all_gather(own_panel, "row", axis=0, tiled=True)
    second = pl.pallas_call(
        functools.partial(exchange_kernel, dests, row_count, 1, False),
        out_shape=inc_shape,
        in_specs=[anyspace],
        out_specs=anyspace,
        scratch_shapes=[dma, dma, dma((2,))],
        compiler_params=pltpu.CompilerParams(has_side_effects=True),
        cost_estimate=cost,
        name="exchange_b",
    )(outgoing)

    group = 16
    with_children = pl.pallas_call(
        functools.partial(assemble_kernel, group, col_tiles),
        out_shape=jax.ShapeDtypeStruct((rows_dev, cols_dev), jnp.float32),
        grid=(dests // group,),
        in_specs=[
            smem,
            pl.BlockSpec((rows_dev, cols_dev), lambda i: (0, 0), pipeline_mode=pl.Buffered(1)),
            pl.BlockSpec((group,) + tile_shape, lambda i: (i, 0, 0)),
            pl.BlockSpec((group,) + tile_shape, lambda i: (i, 0, 0)),
        ],
        out_specs=pl.BlockSpec((rows_dev, cols_dev), lambda i: (0, 0)),
        compiler_params=pltpu.CompilerParams(vmem_limit_bytes=40 << 20),
        name="assemble",
    )(in_labels, update_block[0], first, second)

    columns = lax.dynamic_slice_in_dim(full_panel, col_place * cols_dev, cols_dev, 0)
    half_width = inverse_factor.shape[1] // col_count
    panel_out = lax.dynamic_slice_in_dim(own_panel, col_place * half_width, half_width, 1)[None]
    outer_part = lax.dot_general(
        own_panel,
        columns,
        (((1,), (1,)), ((), ())),
        precision=highest,
        preferred_element_type=jnp.float32,
    )
    updated = with_children - outer_part
    inside = (row_ids[:, None] < live_bound) & (col_ids[None, :] < live_bound)
    schur_out = jnp.where(inside, updated, jnp.zeros_like(updated)).astype(jnp.bfloat16)[None]
    return (schur_out, panel_out)


def solution(mesh):
    return jax.shard_map(
        per_device,
        mesh=mesh,
        in_specs=(
            P("front", "row", "col"),
            P("front", "row", "col"),
            P("front", None, "col"),
            P(("front", "row", "col"), None, None),
            P(("front", "row", "col"), None),
            P(("front", "row", "col")),
            P(("front", "row", "col")),
            P(),
            P("front"),
        ),
        out_specs=(P("front", "row", "col"), P("front", "row", "col")),
        check_vma=False,
    )
```

time: 386 us -> 359 us (0.930)
  Pallas kernels: 0 us -> 316 us
  waiting for transfers between devices: 253 us -> 0.06 us
  local copies, waits for them, and re-layouts: 59 us -> 7.84 us
  starting transfers between devices: 28.2 us -> 0.08 us
  matrix products: 28.2 us -> 19.2 us
    pallas_call x0 -> x4, Pallas kernels: none -> 316 us  [the longest x1 114 us: per_device(): pl.pallas_call(functools.partial(exchange_kernel, dests, row_count, 0, Tr...]
    all_to_all x2 -> x0, waiting for transfers between devices: 186 us -> none  [the longest x1 186 us: per_device(): lax.all_to_all(outgoing.reshape(dest_count, CAP, TILE, TILE), ('front', '...]
    psum x1, waiting for transfers between devices: 67.1 us -> 0.02 us  [per_device(): own_panel = lax.psum(partial_value, 'col')]
    all_to_all x2 -> x0, starting transfers between devices: 28.2 us -> none  [the longest x1 14.6 us: per_device(): lax.all_to_all(outgoing.reshape(dest_count, CAP, TILE, TILE), ('front', '...]
    unnamed x13 -> x12, local copies, waits for them, and re-layouts: 23.7 us -> 6.91 us
    scatter x2 -> x0, local copies, waits for them, and re-layouts: 15.5 us -> none  [the longest x1 14.6 us: per_device(): jnp.zeros((dest_count * CAP, TILE, TILE), jnp.bfloat16).at[position]]
    dot_general x1 -> x0, local copies, waits for them, and re-layouts: 11.9 us -> none  [per_device(): jnp.dot(selector, flat_tiles, preferred_element_type=jnp.float32)]
    dot_general x1 -> x0, matrix products: 7.99 us -> none  [per_device(): jnp.dot(selector, flat_tiles, preferred_element_type=jnp.float32)]
  transfers between devices with their start and end apart: 4 -> 2, of which waited for: 2 -> 0; matrix products, arithmetic and copies ran while one was open for 17% -> 0% of each run, Pallas kernels for 0% -> 88%
where the time goes in v1:
time: 359 us; the launch traced here: 358 us
  Pallas kernels  316 us (88%)
  matrix products  19.2 us (5%)
  between operations  14.9 us (4%)
  local copies, waits for them, and re-layouts  7.84 us (2%)
    pallas_call x1, Pallas kernels, per_device(): pl.pallas_call(functools.partial(exchange_kernel, dests, row_count, 0, Tr...  114 us
    pallas_call x1, Pallas kernels, per_device(): pl.pallas_call(functools.partial(exchange_kernel, dests, row_count, 1, Fa...  105 us
    pallas_call x1, Pallas kernels, per_device(): pl.pallas_call(functools.partial(pack_kernel, dests, row_count, col_tiles...  88.7 us
    dot_general x1, matrix products, per_device(): lax.dot_general(own_panel, columns, (((1,), (1,)), ((), ())), precision=h...  14.2 us
    pallas_call x1, Pallas kernels, per_device(): pl.pallas_call(functools.partial(assemble_kernel, group, col_tiles), out_...  7.77 us
  transfers between devices with their start and end apart: 2, of which 0 were waited for; matrix products, arithmetic and copies ran while one was open for 0% of the time, Pallas kernels for 88%

profile of v1, /device:TPU:1, one launch (start us, length us, event | category | flops | bytes accessed | tf_op | source)
XLA Modules:
  0.0 357.6 jit_solution(6425120529368595145)
XLA Ops:
  7.2 0.0 copy-start
  7.2 0.0 all-reduce.2.cloned.1.call-start
  8.0 0.5 copy-done
  8.5 5.0 %convolution_select_fusion = f32[512,768]{1,0:T(8,128)} fusion(f32[1,768,384]{2,1,0:T(8,128)S(1)} %copy-done, f32[1,512,384]{2,1,0:T(8,128)} %param.10, pred[512]{0:T(512)(128)(4,1)S(1)} %add_compare_fusion.1), kind=kOutput, calls=%fused_computation.4 | convolution fusion | flops 1812332544 | bytes 3539456 | tf_op jit(solution)/shard_map/dot_general | solution.py:146
  13.4 0.0 all-reduce.2.cloned.1.call-update
  13.5 0.0 all-gather.2.cloned.1.call-start
  13.5 88.7 %pack.1 = (bf16[256,128,128]{2,1,0:T(8,128)(2,1)}, s32[128,1,128]{2,1,0:T(1,128)}) custom-call(s32[86]{0:T(128)} %bitcast.15, s32[86]{0:T(128)} %crow.1, s32[86]{0:T(128)} %ccol.1, s32[16]{0:T(128)} %owner.1, bf16[86,128,128]{2,1,0:T(8,128)(2,1)} %tiles.1), custom_call_target="tpu_custom_call" | custom-call | tf_op jit(solution)/shard_map/pack/pallas_call | solution.py:134
  102.2 114.3 %exchange_a.1 = (bf16[128,128,128]{2,1,0:T(8,128)(2,1)}, s32[128,1,128]{2,1,0:T(1,128)}) custom-call(bf16[256,128,128]{2,1,0:T(8,128)(2,1)} %get-tuple-element.14.refs_0_, s32[128,1,128]{2,1,0:T(1,128)} %get-tuple-element.10.refs_1_), custom_call_target="tpu_custom_call" | custom-call | bytes 300000000 | tf_op jit(solution)/shard_map/exchange_a/pallas_call | solution.py:161
  216.5 0.0 all-reduce.2.cloned.1.call-done
  216.5 0.0 all-gather.2.cloned.1.call-update
  216.6 0.0 copy-start.4
  216.6 104.8 %exchange_b.1.second = bf16[128,128,128]{2,1,0:T(8,128)(2,1)} custom-call(bf16[256,128,128]{2,1,0:T(8,128)(2,1)} %get-tuple-element.14.refs_0_), custom_call_target="tpu_custom_call" | custom-call | bytes 300000000 | tf_op jit(solution)/shard_map/exchange_b/pallas_call | solution.py:173
  321.4 0.0 copy-done.4
  321.4 0.0 copy-start.2
  321.4 2.3 copy-done.2
  323.7 0.0 copy-start.3
  323.7 2.2 copy-done.3
  325.9 0.0 copy-start.5
  325.9 7.8 %assemble.1 = f32[512,2048]{1,0:T(8,128)S(1)} custom-call(s32[128,1,128]{2,1,0:T(1,128)S(1)} %copy-done.4, f32[512,2048]{1,0:T(8,128)S(1)} %bitcast.14, bf16[128,128,128]{2,1,0:T(8,128)(2,1)S(1)} %copy-done.3, bf16[128,128,128]{2,1,0:T(8,128)(2,1)} %exchange_b.1.second), custom_call_target="tpu_custom_call" | custom-call | tf_op jit(solution)/shard_map/assemble/pallas_call | solution.py:185
  333.7 0.0 copy-start.1
  333.7 1.9 copy-done.1
  335.6 0.0 copy-done.5
  335.6 0.9 dynamic-slice_bitcast_fusion
  336.6 14.2 %fusion.4 = bf16[1,512,2048]{2,1,0:T(8,128)(2,1)} fusion(f32[512,2048]{1,0:T(8,128)} %copy-done.1, f32[512,768]{1,0:T(8,128)S(1)} %copy-done.5, f32[4096,768]{1,0:T(8,128)} %all-gather.2.cloned.1.call-done, s32[]{:T(128)S(6)} %select_n.15, pred[2048]{0:T(1024)(128)(4,1)S(1)} %add_compare_fusion, pred[512]{0:T(512)(128)(4,1)S(1)} %add_compare_fusion.1), kind=kOutput, calls=%fused_computation.3 | convolution fusion | flops 9667870720 | bytes 14158340 | tf_op jit(solution)/shard_map/dot_general | solution.py:203
  (3 shorter events, 0.0 us)
Async XLA Ops:
  7.2 1.3 copy-start
  7.2 209.4 %all-reduce.2.cloned.1.call-start = ((), (), s32[]{:S(2)}) async-start(), calls=%async_computation | async-start | bytes 3145728 | tf_op jit(solution)/shard_map/psum | solution.py:156
  13.5 323.1 %all-gather.2.cloned.1.call-start = ((), (), s32[]{:S(2)}) async-start(), calls=%async_computation.1 | async-start | bytes 14155776 | tf_op jit(solution)/shard_map/all_gather | solution.py:172
  216.6 104.8 %copy-start.4 = (s32[128,1,128]{2,1,0:T(1,128)S(1)}, s32[128,1,128]{2,1,0:T(1,128)}, u32[]{:S(2)}) copy-start(s32[128,1,128]{2,1,0:T(1,128)} %get-tuple-element.11.lab) | copy-start | bytes 196612
  321.4 2.3 copy-start.2
  323.7 2.2 copy-start.3
  325.9 9.7 %copy-start.5 = (f32[512,768]{1,0:T(8,128)S(1)}, f32[512,768]{1,0:T(8,128)}, u32[]{:S(2)}) copy-start(f32[512,768]{1,0:T(8,128)} %all-reduce.2.cloned.1.call-done) | copy-start | bytes 4718596
  333.7 1.9 copy-start.1
Sparse Core Ops, SparseCore 0:
  13.6 67.0 all-reduce.1
  216.7 107.4 all-gather.1

commit v2 on v0

v2 whole, which is shorter than its diff:
```python
import functools

import jax
import jax.numpy as jnp
from jax import lax
from jax.experimental import pallas as pl
from jax.experimental.pallas import tpu as pltpu
from jax.sharding import PartitionSpec as P

TILE = 128
FEW = 2
CHUNKS = 4
MESH = pl.DeviceIdType.MESH
DMA = pltpu.SemaphoreType.DMA


def index_kernel(fronts, rows_n, col_tiles, target, crow, ccol, owner, idx1, lab1, idx2, code2, idx3, lab3, over, count, few):
    dests = fronts * rows_n
    empty = 4 * col_tiles

    @pl.loop(0, dests)
    def _(i):
        count[i] = 0
        idx1[i] = 0
        idx3[i] = 0
        lab1[i, 0, 0] = empty
        lab3[i, 0, 0] = empty

    @pl.loop(0, fronts)
    def _(f):
        few[f] = 0
        for j in range(FEW):
            idx2[f * FEW + j] = 0
            code2[f, 0, j] = empty * rows_n

    over[0] = 0

    @pl.loop(0, target.shape[0])
    def _(i):
        t = target[i]
        front = owner[t // rows_n]
        row = t % rows_n
        address = front * rows_n + row
        place = crow[i] * col_tiles + ccol[i]
        seen = count[address]
        count[address] = seen + 1

        @pl.when(seen == 0)
        def _():
            idx1[address] = i
            lab1[address, 0, 0] = place

        @pl.when(seen > 0)
        def _():
            k = few[front]
            few[front] = k + 1

            @pl.when(k < FEW)
            def _():
                idx2[front * FEW + k] = i
                code2[front, 0, k] = row * empty + place

            @pl.when(k >= FEW)
            def _():
                idx3[address] = i
                lab3[address, 0, 0] = place
                over[0] = over[0] + 1


def spread_kernel(fronts, rows_n, idx2, code2, tiles, fown, in2, incode, fother, fcols,
                  send2, ts, tr, cs, cr, ys, yr, xs, xr, ks, kr):
    front, row, col = lax.axis_index("front"), lax.axis_index("row"), lax.axis_index("col")
    x, k = row // 2, row % 2
    j = (x + 4 - 2 * col) % 4
    step_rows = fown.shape[0] // CHUNKS

    def at_j(place):
        return (front, ((place + 2 * col) % 4) * 2 + k, col)

    mate = (front, x * 2 + 1 - k, col)
    across = (front, row, 1 - col)

    def part(i):
        return pl.ds(i * step_rows, step_rows)

    def remote(src, dst, ssem, rsem, dev):
        return pltpu.make_async_remote_copy(src, dst, ssem, rsem, device_id=dev, device_id_type=MESH)

    @pl.loop(0, CHUNKS)
    def _(i):
        remote(fown.at[part(i)], fother.at[part(i)], ys, yr.at[i], across).start()

    def give(which, half, i, src, dev):
        b = 2 * which + k
        remote(src, fcols.at[b, half, part(i)], xs, xr.at[which, half, i], dev).start()

    def to_mate(which, half, i, src):
        b = 2 * which + k
        remote(src, fcols.at[b, half, part(i)], ks, kr.at[which], mate).start()

    def own_out(half, i, src):
        @pl.when(j == 0)
        def _():
            give(0, half, i, src, at_j(3))
            give(0, half, i, src, at_j(1))
            to_mate(0, half, i, src)

        @pl.when(j == 1)
        def _():
            give(1, half, i, src, at_j(2))
            give(1, half, i, src, at_j(0))
            to_mate(1, half, i, src)

    @pl.loop(0, CHUNKS)
    def _(i):
        own_out(col, i, fown.at[part(i)])

    for t in range(FEW):
        in2[front * FEW + t] = tiles[idx2[front * FEW + t]]
    incode[front] = code2[front]

    @pl.loop(1, fronts)
    def _(s):
        f = jnp.bitwise_xor(front, (s * 7) % fronts)
        for t in range(FEW):
            send2[f * FEW + t] = tiles[idx2[f * FEW + t]]
        dev = (f, row, col)
        remote(send2.at[pl.ds(f * FEW, FEW)], in2.at[pl.ds(front * FEW, FEW)], ts, tr, dev).start()
        remote(code2.at[f], incode.at[front], cs, cr, dev).start()

    def arrived(which, half, i):
        b = 2 * which + k
        remote(fcols.at[b, half, part(i)], fcols.at[b, half, part(i)], xs, xr.at[which, half, i], mate).wait_recv()

    def pass_on(which, half, i, dev):
        b = 2 * which + k
        src = fcols.at[b, half, part(i)]
        if dev is not None:
            give(which, half, i, src, dev)
        to_mate(which, half, i, src)

    @pl.loop(0, 2 * CHUNKS + 1)
    def _(s):
        @pl.when(s < 2 * CHUNKS)
        def _():
            late = s // CHUNKS
            half = (col + late) % 2
            i = s % CHUNKS

            @pl.when(late == 1)
            def _():
                remote(fown.at[part(i)], fother.at[part(i)], ys, yr.at[i], across).wait_recv()
                own_out(half, i, fother.at[part(i)])

            @pl.when(j == 0)
            def _():
                arrived(1, half, i)
                pass_on(1, half, i, None)

            @pl.when(j == 1)
            def _():
                arrived(0, half, i)
                pass_on(0, half, i, None)

            @pl.when(j == 2)
            def _():
                arrived(1, half, i)
                pass_on(1, half, i, at_j(3))

            @pl.when(j == 3)
            def _():
                arrived(0, half, i)
                pass_on(0, half, i, at_j(2))

        @pl.when(s > 0)
        def _():
            half = (col + (s - 1) // CHUNKS) % 2
            i = (s - 1) % CHUNKS

            @pl.when(j == 2)
            def _():
                arrived(0, half, i)
                pass_on(0, half, i, None)

            @pl.when(j == 3)
            def _():
                arrived(1, half, i)
                pass_on(1, half, i, None)

    @pl.when(j < 2)
    def _():
        b = 2 * j + k
        fcols[b, col] = fown[...]
        fcols[b, 1 - col] = fother[...]

    remote(fown, fother, ys, yr.at[0], across).wait_send()
    pairs = fcols.at[pl.ds(0, 2)]
    remote(pairs, pairs, ks, kr.at[0], mate).wait_send()
    for which in range(2):
        b = 2 * which + 1 - k
        remote(fcols.at[b], fcols.at[b], ks, kr.at[which], mate).wait_recv()

    @pl.when(j < 2)
    def _():
        remote(pairs, pairs, xs, kr.at[0], mate).wait_send()

    @pl.when(j >= 2)
    def _():
        remote(fcols.at[0], fcols.at[0], xs, kr.at[0], mate).wait_send()

    some = pl.ds(0, (fronts - 1) * FEW)
    both = remote(send2.at[some], in2.at[some], ts, tr, mate)
    both.wait_send()
    both.wait_recv()
    most = pl.ds(0, fronts - 1)
    codes = remote(code2.at[most], incode.at[most], cs, cr, mate)
    codes.wait_send()
    codes.wait_recv()


def exchange_kernel(fronts, rows_n, hop, *refs):
    if hop:
        (idx, lab, tiles, code, codes_out, in2, inc, inlab, xin, xcodes,
         send, xsend, ssem, rsem, lssem, lrsem, xssem, xrsem, cssem, crsem, lsem) = refs
    else:
        idx, lab, tiles, inc, inlab, send, ssem, rsem, lssem, lrsem, lsem = refs
    dests = fronts * rows_n
    front, row, col = lax.axis_index("front"), lax.axis_index("row"), lax.axis_index("col")
    me = front * rows_n + row
    empty = 4 * 16

    def remote(src, dst, s, r, dev):
        return pltpu.make_async_remote_copy(src, dst, s, r, device_id=dev, device_id_type=MESH)

    def pack_row(r):
        @pl.loop(0, fronts)
        def _(g):
            t = jnp.where(code[g, 0, 1] // empty == r, 1, 0)
            xsend[r * fronts + g] = in2[g * FEW + t]

    send[me] = tiles[idx[me]]
    own = pltpu.make_async_copy(send.at[me], inc.at[me], lsem.at[0])
    own.start()
    ownlab = pltpu.make_async_copy(lab.at[me], inlab.at[me], lsem.at[1])
    ownlab.start()
    per = dests // rows_n

    @pl.loop(0, rows_n)
    def _(outer):
        @pl.loop(0, per)
        def _(inner):
            step = outer * per + inner

            @pl.when(step > 0)
            def _():
                p = jnp.bitwise_xor(me, (step * 37) % dests)
                dev = (p // rows_n, p % rows_n, col)
                send[p] = tiles[idx[p]]
                remote(send.at[p], inc.at[me], ssem, rsem, dev).start()
                remote(lab.at[p], inlab.at[me], lssem, lrsem, dev).start()

        if hop:
            @pl.when(outer > 0)
            def _():
                r = jnp.bitwise_xor(row, outer)
                pack_row(r)
                dev = (front, r, col)
                remote(xsend.at[pl.ds(r * fronts, fronts)], xin.at[pl.ds(row * fronts, fronts)], xssem, xrsem, dev).start()
                remote(codes_out, xcodes.at[row], cssem, crsem, dev).start()

    if hop:
        pack_row(row)
        mine = pl.ds(row * fronts, fronts)
        ownx = pltpu.make_async_copy(xsend.at[mine], xin.at[mine], lsem.at[2])
        ownx.start()
        ownc = pltpu.make_async_copy(codes_out, xcodes.at[row], lsem.at[3])
        ownc.start()
    own.wait()
    ownlab.wait()
    here = (front, row, col)
    some = pl.ds(0, dests - 1)
    both = remote(send.at[some], inc.at[some], ssem, rsem, here)
    both.wait_send()
    both.wait_recv()
    labs = remote(lab.at[some], inlab.at[some], lssem, lrsem, here)
    labs.wait_send()
    labs.wait_recv()
    if hop:
        ownx.wait()
        ownc.wait()
        some = pl.ds(0, (rows_n - 1) * fronts)
        xs = remote(xsend.at[some], xin.at[some], xssem, xrsem, here)
        xs.wait_send()
        xs.wait_recv()
        some = pl.ds(0, rows_n - 1)
        cs = remote(xcodes.at[some], xcodes.at[some], cssem, crsem, here)
        cs.wait_send()
        cs.wait_recv()


def add_tile(out, place, col_tiles, tile):
    @pl.when(place < 4 * col_tiles)
    def _():
        r = pl.multiple_of((place // col_tiles) * TILE, TILE)
        c = pl.multiple_of((place % col_tiles) * TILE, TILE)
        out[pl.ds(r, TILE), pl.ds(c, TILE)] += tile[...].astype(jnp.float32)


def more_kernel(group, col_tiles, lab, base, tiles, out):
    step = pl.program_id(0)

    @pl.when(step == 0)
    def _():
        out[...] = base[...]

    @pl.loop(0, group)
    def _(i):
        add_tile(out, lab[step * group + i, 0, 0], col_tiles, tiles.at[i])


def finish_kernel(group, col_tiles, steps, lab, code, live, base, first, second, out, total):
    step = pl.program_id(0)
    row, col = lax.axis_index("row"), lax.axis_index("col")
    empty = 4 * col_tiles

    @pl.when(step == 0)
    def _():
        total[...] = base[...]

    @pl.loop(0, group)
    def _(i):
        add_tile(total, lab[step * group + i, 0, 0], col_tiles, first.at[i])
        c0 = code[step, i, 0, 0]
        c1 = code[step, i, 0, 1]
        place = jnp.where(c1 // empty == row, c1 % empty, empty)
        place = jnp.where(c0 // empty == row, c0 % empty, place)
        add_tile(total, place, col_tiles, second.at[i])

    @pl.when(step == steps - 1)
    def _():
        bound = live[0] * TILE
        height, width = total.shape

        @pl.loop(0, height // TILE)
        def _(i):
            rows = pl.ds(pl.multiple_of(i * TILE, TILE), TILE)
            row_ids = row * height + i * TILE + lax.broadcasted_iota(jnp.int32, (TILE, width), 0)
            col_ids = col * width + lax.broadcasted_iota(jnp.int32, (TILE, width), 1)
            inside = (row_ids < bound) & (col_ids < bound)
            out[rows] = jnp.where(inside, total[rows], 0.0).astype(out.dtype)


def per_device(
    update_block,
    front_panel,
    inverse_factor,
    child_tiles,
    child_target,
    child_row,
    child_col,
    front_owner,
    live_tiles,
):
    highest = lax.Precision.HIGHEST
    rows_dev = update_block.shape[1]
    cols_dev = update_block.shape[2]
    fronts = lax.axis_size("front")
    rows_n = lax.axis_size("row")
    row_place = lax.axis_index("row")
    col_place = lax.axis_index("col")
    dests = fronts * rows_n
    col_tiles = cols_dev // TILE
    half = front_panel.shape[2]

    anyspace = pl.BlockSpec(memory_space=pl.ANY)
    smem = pl.BlockSpec(memory_space=pltpu.SMEM)
    vmem = pl.BlockSpec(memory_space=pltpu.VMEM)
    shape = jax.ShapeDtypeStruct
    tile_shape = (TILE, TILE)
    ints = lambda *s: shape(s, jnp.int32)
    params = pltpu.CompilerParams(has_side_effects=True, vmem_limit_bytes=40 << 20)

    idx1, lab1, idx2, code2, idx3, lab3, over = pl.pallas_call(
        functools.partial(index_kernel, fronts, rows_n, col_tiles),
        out_shape=(ints(dests), ints(dests, 1, 128), ints(fronts * FEW), ints(fronts, 1, 128),
                   ints(dests), ints(dests, 1, 128), ints(1)),
        in_specs=[smem] * 4,
        out_specs=(smem,) * 7,
        scratch_shapes=[pltpu.SMEM((dests,), jnp.int32), pltpu.SMEM((fronts,), jnp.int32)],
        name="index",
    )(child_target[:, 0], child_row, child_col, front_owner)

    factor = lax.all_gather(inverse_factor[0], "col", axis=1, tiled=True)
    over_all = lax.psum(over.astype(jnp.float32), ("front", "row", "col"))

    in2, incode, fother, fcols = pl.pallas_call(
        functools.partial(spread_kernel, fronts, rows_n),
        out_shape=(shape((fronts * FEW,) + tile_shape, jnp.bfloat16), ints(fronts, 1, 128),
                   shape((rows_dev, half), jnp.float32), shape((4, 2, rows_dev, half), jnp.float32)),
        in_specs=[smem, vmem, vmem, vmem],
        out_specs=(vmem,) * 4,
        scratch_shapes=[pltpu.VMEM((fronts * FEW,) + tile_shape, jnp.bfloat16)] + [DMA] * 5
        + [DMA((CHUNKS,)), DMA, DMA((2, 2, CHUNKS)), DMA, DMA((2,))],
        compiler_params=params,
        cost_estimate=pl.CostEstimate(flops=0, bytes_accessed=150_000_000, transcendentals=0),
        name="spread",
    )(idx2, code2, child_tiles, front_panel[0])

    inc_shape = shape((dests,) + tile_shape, jnp.bfloat16)
    send_buf = pltpu.VMEM((dests,) + tile_shape, jnp.bfloat16)
    first, in_labels, second, in_codes = pl.pallas_call(
        functools.partial(exchange_kernel, fronts, rows_n, True),
        out_shape=(inc_shape, ints(dests, 1, 128), inc_shape, ints(rows_n, fronts, 1, 128)),
        in_specs=[smem, anyspace, vmem, smem, anyspace, vmem],
        out_specs=(anyspace,) * 4,
        scratch_shapes=[send_buf, send_buf] + [DMA] * 8 + [DMA((4,))],
        compiler_params=params,
        cost_estimate=pl.CostEstimate(flops=0, bytes_accessed=300_000_000, transcendentals=0),
        name="exchange",
    )(idx1, lab1, child_tiles, incode, incode, in2)

    live_bound = live_tiles[0] * TILE
    row_ids = row_place * rows_dev + jnp.arange(rows_dev, dtype=jnp.int32)
    col_row_ids = col_place * cols_dev + jnp.arange(cols_dev, dtype=jnp.int32)

    def rows_of(left, right, ids):
        dims = (((1,), (1,)), ((), ()))
        value = lax.dot_general(left, factor[:, :half], dims, precision=highest, preferred_element_type=jnp.float32)
        value += lax.dot_general(right, factor[:, half:], dims, precision=highest, preferred_element_type=jnp.float32)
        return jnp.where(ids[:, None] < live_bound, value, jnp.zeros_like(value))

    mine = front_panel[0]
    swap = col_place == 1
    own_panel = rows_of(jnp.where(swap, fother, mine), jnp.where(swap, mine, fother), row_ids)
    columns = rows_of(fcols[:, 0].reshape(cols_dev, half), fcols[:, 1].reshape(cols_dev, half), col_row_ids)
    panel_out = lax.dynamic_slice_in_dim(own_panel, col_place * half, half, 1)[None]
    base = update_block[0] - lax.dot_general(
        own_panel, columns, (((1,), (1,)), ((), ())), precision=highest, preferred_element_type=jnp.float32
    )

    block = (rows_dev, cols_dev)
    group = dests // rows_n
    whole = pl.BlockSpec(block, lambda i: (0, 0), pipeline_mode=pl.Buffered(1))
    tiles_spec = pl.BlockSpec((group,) + tile_shape, lambda i: (i, 0, 0))

    def further(value):
        tiles3, labels3 = pl.pallas_call(
            functools.partial(exchange_kernel, fronts, rows_n, False),
            out_shape=(inc_shape, ints(dests, 1, 128)),
            in_specs=[smem, anyspace, vmem],
            out_specs=(anyspace,) * 2,
            scratch_shapes=[send_buf] + [DMA] * 4 + [DMA((4,))],
            compiler_params=params,
            name="further",
        )(idx3, lab3, child_tiles)
        return pl.pallas_call(
            functools.partial(more_kernel, group, col_tiles),
            out_shape=shape(block, jnp.float32),
            grid=(rows_n,),
            in_specs=[smem, whole, tiles_spec],
            out_specs=pl.BlockSpec(block, lambda i: (0, 0)),
            compiler_params=pltpu.CompilerParams(vmem_limit_bytes=40 << 20),
            name="more",
        )(labels3, value, tiles3)

    base = lax.cond(over_all[0] > 0, further, lambda value: value, base)

    schur_out = pl.pallas_call(
        functools.partial(finish_kernel, group, col_tiles, rows_n),
        out_shape=shape(block, jnp.bfloat16),
        grid=(rows_n,),
        in_specs=[smem, smem, smem, whole, tiles_spec, tiles_spec],
        out_specs=pl.BlockSpec(block, lambda i: (0, 0)),
        scratch_shapes=[pltpu.VMEM(block, jnp.float32)],
        compiler_params=pltpu.CompilerParams(vmem_limit_bytes=40 << 20),
        name="finish",
    )(in_labels, in_codes, live_tiles, base, first, second)[None]
    return (schur_out, panel_out)


def solution(mesh):
    return jax.shard_map(
        per_device,
        mesh=mesh,
        in_specs=(
            P("front", "row", "col"),
            P("front", "row", "col"),
            P("front", None, "col"),
            P(("front", "row", "col"), None, None),
            P(("front", "row", "col"), None),
            P(("front", "row", "col")),
            P(("front", "row", "col")),
            P(),
            P("front"),
        ),
        out_specs=(P("front", "row", "col"), P("front", "row", "col")),
        check_vma=False,
    )
```

time: 386 us -> 459 us (1.19)
  Pallas kernels: 0 us -> 300 us
  waiting for transfers between devices: 253 us -> 0.68 us
  blocking collectives: 0 us -> 81.3 us
  local copies, waits for them, and re-layouts: 59 us -> 17.1 us
  starting transfers between devices: 28.2 us -> 0.04 us
  matrix products: 28.2 us -> 43 us
    pallas_call x0 -> x6, Pallas kernels: none -> 300 us  [the longest x1 116 us: per_device(): pl.pallas_call(functools.partial(exchange_kernel, fronts, rows_n, True),...]
    all_to_all x2 -> x0, waiting for transfers between devices: 186 us -> none  [the longest x1 186 us: per_device(): lax.all_to_all(outgoing.reshape(dest_count, CAP, TILE, TILE), ('front', '...]
    psum x0 -> x1, blocking collectives: none -> 81.3 us  [per_device(): over_all = lax.psum(over.astype(jnp.float32), ('front', 'row', 'col'))]
    psum x1 -> x0, waiting for transfers between devices: 67.1 us -> none  [per_device(): own_panel = lax.psum(partial_value, 'col')]
    all_to_all x2 -> x0, starting transfers between devices: 28.2 us -> none  [the longest x1 14.6 us: per_device(): lax.all_to_all(outgoing.reshape(dest_count, CAP, TILE, TILE), ('front', '...]
    dot_general x2 -> x4, matrix products: 13 us -> 29 us  [the longest x2 15.7 us: rows_of(): lax.dot_general(left, factor[:, :half], dims, precision=highest, preferre...]
    scatter x2 -> x0, local copies, waits for them, and re-layouts: 15.5 us -> none  [the longest x1 14.6 us: per_device(): jnp.zeros((dest_count * CAP, TILE, TILE), jnp.bfloat16).at[position]]
    unnamed x13 -> x28, local copies, waits for them, and re-layouts: 23.7 us -> 10.8 us
  transfers between devices with their start and end apart: 4 -> 1, of which waited for: 2 -> 0; matrix products, arithmetic and copies ran while one was open for 17% -> 1% of each run, Pallas kernels for 0% -> 38%
where the time goes in v2:
time: 459 us
  Pallas kernels  300 us (65%)
  blocking collectives  81.3 us (18%)
  matrix products  43 us (9%)
  local copies, waits for them, and re-layouts  17.1 us (4%)
  between operations  16.1 us (4%)
    pallas_call x1, Pallas kernels, per_device(): pl.pallas_call(functools.partial(exchange_kernel, fronts, rows_n, True),...  116 us
    pallas_call x1, Pallas kernels, further(): pl.pallas_call(functools.partial(exchange_kernel, fronts, rows_n, False),...  108 us
    psum x1, blocking collectives, per_device(): over_all = lax.psum(over.astype(jnp.float32), ('front', 'row', 'col'))  81.3 us
    pallas_call x1, Pallas kernels, per_device(): pl.pallas_call(functools.partial(spread_kernel, fronts, rows_n), out_shap...  52.1 us
    dot_general x2, matrix products, rows_of(): lax.dot_general(left, factor[:, :half], dims, precision=highest, preferre...  15.7 us
    dot_general x1, matrix products, per_device(): lax.dot_general(own_panel, columns, (((1,), (1,)), ((), ())), precision=h...  14 us
    dot_general x2, matrix products, rows_of(): lax.dot_general(right, factor[:, half:], dims, precision=highest, preferr...  13.3 us
    unnamed x28, local copies, waits for them, and re-layouts  10.8 us
  transfers between devices with their start and end apart: 1, of which 0 were waited for; matrix products, arithmetic and copies ran while one was open for 1% of the time, Pallas kernels for 38%

profile of v2, /device:TPU:1, one launch (start us, length us, event | category | flops | bytes accessed | tf_op | source)
XLA Modules:
  0.0 458.7 jit_solution(3007049217967248892)
XLA Ops:
  7.2 0.7 all-gather.3.cloned.1.call-update
  7.9 7.8 %index.1 = (s32[128]{0:T(128)}, s32[128,1,128]{2,1,0:T(1,128)}, s32[32]{0:T(128)}, s32[16,1,128]{2,1,0:T(1,128)}, s32[128]{0:T(128)S(1)}, /*index=5*/s32[128,1,128]{2,1,0:T(1,128)S(1)}, s32[1]{0:T(128)}) custom-call(s32[86]{0:T(128)} %bitcast.31, s32[86]{0:T(128)} %crow.1, s32[86]{0:T(128)} %ccol.1, s32[16]{0:T(128)} %owner.1), custom_call_target="tpu_custom_call" | custom-call | tf_op jit(solution)/shard_map/index/pallas_call | solution.py:383
  16.3 81.3 %psum.7 = f32[1]{0:T(128)} all-reduce(f32[1]{0:T(128)S(6)} %convert_element_type.9), channel_id=1, replica_groups=mesh['front'=16,'row'=8,'col'=2] {'front','row','col'}, use_global_device_ids=true, to_apply=%region_0.0 | all-reduce | flops 1 | bytes 8 | tf_op jit(solution)/shard_map/psum | solution.py:394
  98.9 1.1 copy-done
  100.1 0.7 copy-done.7
  100.8 0.6 copy-done.9
  101.4 52.1 %spread.1 = (bf16[32,128,128]{2,1,0:T(8,128)(2,1)S(1)}, s32[16,1,128]{2,1,0:T(1,128)S(1)}, f32[512,384]{1,0:T(8,128)S(1)}, f32[4,2,512,384]{3,2,1,0:T(8,128)S(1)}) custom-call(s32[32]{0:T(128)S(1)} %copy-done.9, s32[16,1,128]{2,1,0:T(1,128)S(1)} %copy-done.7, bf16[86,128,128]{2,1,0:T(8,128)(2,1)} %refs_2_.1, f32[512,384]{1,0:T(8,128)S(1)} %bitcast.23), custom_call_target="tpu_custom_call" | custom-call | bytes 150000000 | tf_op jit(solution)/shard_map/spread/pallas_call | solution.py:396
  153.5 115.6 %exchange.1 = (bf16[128,128,128]{2,1,0:T(8,128)(2,1)S(1)}, s32[128,1,128]{2,1,0:T(1,128)S(1)}, bf16[128,128,128]{2,1,0:T(8,128)(2,1)S(1)}, s32[8,16,1,128]{3,2,1,0:T(1,128)S(1)}) custom-call(s32[128]{0:T(128)S(1)} %copy-done.8, s32[128,1,128]{2,1,0:T(1,128)S(1)} %copy-done.6, bf16[86,128,128]{2,1,0:T(8,128)(2,1)S(1)} %copy-done.10, ...), custom_call_target="tpu_custom_call" | custom-call | bytes 300000000 | tf_op jit(solution)/shard_map/exchange/pallas_call | solution.py:411
  269.1 1.9 copy-done.2
  271.0 2.0 copy-done.4
  273.1 3.2 fusion.21
  276.2 12.7 %fusion.10 = f32[2048,768]{1,0:T(8,128)S(1)} fusion(f32[2048,384]{1,0:T(8,128)} %bitcast.25, f32[768,768]{1,0:T(8,128)} %bitcast.26), kind=kOutput, calls=%fused_computation.10 | convolution fusion | flops 7247757312 | bytes 10616832 | tf_op jit(solution)/shard_map/dot_general | solution.py:428
  289.0 10.5 %fusion.7 = f32[2048,768]{1,0:T(8,128)S(1)} fusion(f32[2048,384]{1,0:T(8,128)S(1)} %bitcast.24, f32[768,768]{1,0:T(8,128)S(1)} %bitcast.27), kind=kOutput, calls=%fused_computation.7 | convolution fusion | flops 7247757312 | bytes 10616832 | tf_op jit(solution)/shard_map/dot_general | solution.py:429
  299.6 3.0 fusion.12
  302.5 2.7 add_select_fusion
  305.3 0.9 dynamic-slice_bitcast_fusion
  306.2 14.0 %bitcast_subtract_fusion = f32[512,2048]{1,0:T(8,128)} fusion(f32[1,512,2048]{2,1,0:T(8,128)} %param.11, f32[512,768]{1,0:T(8,128)S(1)} %add_select_fusion, f32[2048,768]{1,0:T(8,128)S(1)} %fusion.10, f32[2048,768]{1,0:T(8,128)S(1)} %fusion.7, pred[2048]{0:T(1024)(128)(4,1)S(1)} %add_compare_fusion), kind=kOutput, calls=%fused_computation.3 | convolution fusion | flops 9667870720 | bytes 22546432 | tf_op jit(solution)/shard_map/dot_general | solution.py:437
  320.2 116.5 %conditional.1 = (f32[512,2048]{1,0:T(8,128)}) conditional(s32[]{:T(128)} %bitcast.2, f32[512,2048]{1,0:T(8,128)} %bitcast_subtract_fusion, (s32[128]{0:T(128)S(1)}, s32[128,1,128]{2,1,0:T(1,128)S(1)}, bf16[86,128,128]{2,1,0:T(8,128)(2,1)S(1)}, f32[512,2048]{1,0:T(8,128)}) %tuple.21), branch_computations={%region_1.2_spmd, %region_2.3_spmd} | conditional | bytes 8388616 | solution.py:466
  320.2 108.3 %further.1 = (bf16[128,128,128]{2,1,0:T(8,128)(2,1)S(1)}, s32[128,1,128]{2,1,0:T(1,128)S(1)}) custom-call(s32[128]{0:T(128)S(1)} %get-tuple-element.12.refs_0_, s32[128,1,128]{2,1,0:T(1,128)S(1)} %get-tuple-element.13.refs_1_, bf16[86,128,128]{2,1,0:T(8,128)(2,1)S(1)} %get-tuple-element.14.refs_2_), custom_call_target="tpu_custom_call" | custom-call | tf_op jit(solution)/shard_map/cond/branch_1_fun/further/pallas_call | solution.py:447
  428.6 2.2 copy.15.base
  430.8 6.0 %more.1 = f32[512,2048]{1,0:T(8,128)} custom-call(s32[128,1,128]{2,1,0:T(1,128)S(1)} %get-tuple-element.15.lab, f32[512,2048]{1,0:T(8,128)S(1)} %copy.15.base, bf16[128,128,128]{2,1,0:T(8,128)(2,1)S(1)} %get-tuple-element.17.tiles), custom_call_target="tpu_custom_call" | custom-call | tf_op jit(solution)/shard_map/cond/branch_1_fun/more/pallas_call | solution.py:456
  436.7 2.2 copy-done.3
  438.9 2.2 copy-done.5
  441.1 10.8 %finish.1 = bf16[512,2048]{1,0:T(8,128)(2,1)} custom-call(s32[128,1,128]{2,1,0:T(1,128)S(1)} %get-tuple-element.41.lab, s32[8,16,1,128]{3,2,1,0:T(1,128)S(1)} %get-tuple-element.42.code, s32[1]{0:T(128)S(6)} %copy.14.live, f32[512,2048]{1,0:T(8,128)} %get-tuple-element.52.base, bf16[128,128,128]{2,1,0:T(8,128)(2,1)S(1)} %copy-done.3, ...), custom_call_target="tpu_custom_call" | custom-call | tf_op jit(solution)/shard_map/finish/pallas_call | solution.py:468
  (25 shorter events, 0.1 us)
Async XLA Ops:
  7.2 269.1 %all-gather.3.cloned.1.call-start = ((), (), s32[]{:S(2)}) async-start(), calls=%async_computation | async-start | bytes 3538944 | tf_op jit(solution)/shard_map/all_gather | solution.py:393
  15.7 137.8 %copy-start.8 = (s32[128]{0:T(128)S(1)}, s32[128]{0:T(128)}, u32[]{:S(2)}) copy-start(s32[128]{0:T(128)} %get-tuple-element.35.refs_0_) | copy-start | bytes 1540
  98.9 1.1 copy-start
  100.1 0.7 copy-start.7
  100.8 0.6 copy-start.9
  101.4 52.1 %copy-start.6 = (s32[128,1,128]{2,1,0:T(1,128)S(1)}, s32[128,1,128]{2,1,0:T(1,128)}, u32[]{:S(2)}) copy-start(s32[128,1,128]{2,1,0:T(1,128)} %get-tuple-element.36.refs_1_) | copy-start | bytes 196612
  101.4 52.1 %copy-start.10 = (bf16[86,128,128]{2,1,0:T(8,128)(2,1)S(1)}, bf16[86,128,128]{2,1,0:T(8,128)(2,1)}, u32[]{:S(2)}) copy-start(bf16[86,128,128]{2,1,0:T(8,128)(2,1)} %refs_2_.1) | copy-start | bytes 8454148
  269.1 1.9 copy-start.2
  271.0 2.0 copy-start.4
  276.2 12.8 %copy-start.12 = (f32[4,1,512,384]{3,2,1,0:T(8,128)S(1)}, f32[4,1,512,384]{3,2,1,0:T(8,128)}, u32[]{:S(2)}) copy-start(f32[4,1,512,384]{3,2,1,0:T(8,128)} %get-tuple-element.50) | copy-start | bytes 9437188
  276.2 12.8 %copy-start.13 = (f32[1,768,768]{2,1,0:T(8,128)S(1)}, f32[1,768,768]{2,1,0:T(8,128)}, u32[]{:S(2)}) copy-start(f32[1,768,768]{2,1,0:T(8,128)} %all-gather.3.cloned.1.call-done) | copy-start | bytes 7077892
  289.0 10.6 %copy-start.1 = (f32[1,512,384]{2,1,0:T(8,128)S(1)}, f32[1,512,384]{2,1,0:T(8,128)}, u32[]{:S(2)}) copy-start(f32[1,512,384]{2,1,0:T(8,128)} %param.12) | copy-start | bytes 2359300
  306.2 14.0 %copy-start.11 = (bf16[86,128,128]{2,1,0:T(8,128)(2,1)S(1)}, bf16[86,128,128]{2,1,0:T(8,128)(2,1)}, u32[]{:S(2)}) copy-start(bf16[86,128,128]{2,1,0:T(8,128)(2,1)} %refs_2_.1) | copy-start | bytes 8454148
  436.7 2.2 copy-start.3
  438.9 2.2 copy-start.5
Sparse Core Ops, SparseCore 0:
  9.8 45.5 all-gather.2

commit v3 on v2

--- a/solution.py
+++ b/solution.py
@@ -8,13 +8,13 @@
 from jax.sharding import PartitionSpec as P
 
 TILE = 128
-FEW = 2
+FEW = 3
 CHUNKS = 4
 MESH = pl.DeviceIdType.MESH
 DMA = pltpu.SemaphoreType.DMA
 
 
-def index_kernel(fronts, rows_n, col_tiles, target, crow, ccol, owner, idx1, lab1, idx2, code2, idx3, lab3, over, count, few):
+def index_kernel(fronts, rows_n, col_tiles, target, crow, ccol, owner, idx1, lab1, idx2, code2, idx3, lab3, count, few, over):
     dests = fronts * rows_n
     empty = 4 * col_tiles
 
@@ -65,6 +65,10 @@
                 idx3[address] = i
                 lab3[address, 0, 0] = place
                 over[0] = over[0] + 1
+
+    @pl.loop(0, fronts)
+    def _(f):
+        code2[f, 0, FEW] = over[0]
 
 
 def spread_kernel(fronts, rows_n, idx2, code2, tiles, fown, in2, incode, fother, fcols,
@@ -218,10 +222,48 @@
     codes.wait_recv()
 
 
+def schur_base(live, fown, fother, fcols, factor, update, own_panel, base, panel):
+    row, col = lax.axis_index("row"), lax.axis_index("col")
+    height, width = base.shape
+    half = fown.shape[1]
+    step = height // 2
+    bound = live[0] * TILE
+    mine = pl.ds(pl.multiple_of(col * half, TILE), half)
+    theirs = pl.ds(pl.multiple_of((1 - col) * half, TILE), half)
+
+    def times(a, b):
+        return lax.dot_general(
+            a, b, (((1,), (1,)), ((), ())), precision=lax.Precision.HIGHEST, preferred_element_type=jnp.float32
+        )
+
+    def panel_rows(a, a_part, b, b_part, start):
+        value = times(a, factor[:, a_part]) + times(b, factor[:, b_part])
+        ids = start + lax.broadcasted_iota(jnp.int32, value.shape, 0)
+        return jnp.where(ids < bound, value, 0.0)
+
+    @pl.loop(0, 2)
+    def _(i):
+        rows = pl.ds(pl.multiple_of(i * step, step), step)
+        own_panel[rows] = panel_rows(fown[rows], mine, fother[rows], theirs, row * height + i * step)
+
+    panel[...] = own_panel[:, mine]
+
+    @pl.loop(0, width // step)
+    def _(c):
+        rows = pl.ds(pl.multiple_of((c % 2) * step, step), step)
+        value = panel_rows(
+            fcols[c // 2, 0, rows], pl.ds(0, half), fcols[c // 2, 1, rows], pl.ds(half, half), col * width + c * step
+        )
+        lanes = pl.ds(pl.multiple_of(c * step, step), step)
+        base[:, lanes] = update[:, lanes] - times(own_panel[...], value)
+
+
 def exchange_kernel(fronts, rows_n, hop, *refs):
     if hop:
-        (idx, lab, tiles, code, codes_out, in2, inc, inlab, xin, xcodes,
-         send, xsend, ssem, rsem, lssem, lrsem, xssem, xrsem, cssem, crsem, lsem) = refs
+        (idx, lab, tiles, code, codes_out, in2, live, fown, fother, fcols, factor, update,
+         inc, inlab, xin, xcodes, ycodes, over, base, panel,
+         send, xsend, old, own_panel,
+         ssem, rsem, lssem, lrsem, xssem, xrsem, cssem, crsem, yssem, yrsem, lsem) = refs
     else:
         idx, lab, tiles, inc, inlab, send, ssem, rsem, lssem, lrsem, lsem = refs
     dests = fronts * rows_n
@@ -235,9 +277,14 @@
     def pack_row(r):
         @pl.loop(0, fronts)
         def _(g):
-            t = jnp.where(code[g, 0, 1] // empty == r, 1, 0)
+            t = 0
+            for k in range(1, FEW):
+                t = jnp.where(code[g, 0, k] // empty == r, k, t)
             xsend[r * fronts + g] = in2[g * FEW + t]
 
+    if hop:
+        fetch = pltpu.make_async_copy(update, old, lsem.at[4])
+        fetch.start()
     send[me] = tiles[idx[me]]
     own = pltpu.make_async_copy(send.at[me], inc.at[me], lsem.at[0])
     own.start()
@@ -267,6 +314,9 @@
                 dev = (front, r, col)
                 remote(xsend.at[pl.ds(r * fronts, fronts)], xin.at[pl.ds(row * fronts, fronts)], xssem, xrsem, dev).start()
                 remote(codes_out, xcodes.at[row], cssem, crsem, dev).start()
+
+            other = (front, jnp.bitwise_xor(row, outer), 1 - col)
+            remote(codes_out, ycodes.at[row], yssem, yrsem, other).start()
 
     if hop:
         pack_row(row)
@@ -275,6 +325,8 @@
         ownx.start()
         ownc = pltpu.make_async_copy(codes_out, xcodes.at[row], lsem.at[3])
         ownc.start()
+        fetch.wait()
+        schur_base(live, fown, fother, fcols, factor, old, own_panel, base, panel)
     own.wait()
     ownlab.wait()
     here = (front, row, col)
@@ -296,6 +348,11 @@
         cs = remote(xcodes.at[some], xcodes.at[some], cssem, crsem, here)
         cs.wait_send()
         cs.wait_recv()
+        ys = remote(ycodes, ycodes, yssem, yrsem, here)
+        ys.wait_send()
+        ys.wait_recv()
+        counts = jnp.sum(xcodes[...] + ycodes[...], axis=0)
+        over[...] = jnp.sum(counts, axis=0)
 
 
 def add_tile(out, place, col_tiles, tile):
@@ -318,11 +375,13 @@
         add_tile(out, lab[step * group + i, 0, 0], col_tiles, tiles.at[i])
 
 
-def finish_kernel(group, col_tiles, steps, lab, code, live, base, first, second, out, total):
+def finish_kernel(group, col_tiles, steps, lab, code, live, base, first, second, panel_in, out, panel_out, total):
     step = pl.program_id(0)
     row, col = lax.axis_index("row"), lax.axis_index("col")
     empty = 4 * col_tiles
 
+    panel_out[...] = panel_in[...]
+
     @pl.when(step == 0)
     def _():
         total[...] = base[...]
@@ -330,10 +389,10 @@
     @pl.loop(0, group)
     def _(i):
         add_tile(total, lab[step * group + i, 0, 0], col_tiles, first.at[i])
-        c0 = code[step, i, 0, 0]
-        c1 = code[step, i, 0, 1]
-        place = jnp.where(c1 // empty == row, c1 % empty, empty)
-        place = jnp.where(c0 // empty == row, c0 % empty, place)
+        place = empty
+        for k in range(FEW):
+            c = code[step, i, 0, k]
+            place = jnp.where(c // empty == row, c % empty, place)
         add_tile(total, place, col_tiles, second.at[i])
 
     @pl.when(step == steps - 1)
@@ -361,18 +420,16 @@
     front_owner,
     live_tiles,
 ):
-    highest = lax.Precision.HIGHEST
     rows_dev = update_block.shape[1]
     cols_dev = update_block.shape[2]
     fronts = lax.axis_size("front")
     rows_n = lax.axis_size("row")
-    row_place = lax.axis_index("row")
-    col_place = lax.axis_index("col")
     dests = fronts * rows_n
     col_tiles = cols_dev // TILE
     half = front_panel.shape[2]
 
     anyspace = pl.BlockSpec(memory_space=pl.ANY)
+    hbm = pl.BlockSpec(memory_space=pltpu.HBM)
     smem = pl.BlockSpec(memory_space=pltpu.SMEM)
     vmem = pl.BlockSpec(memory_space=pltpu.VMEM)
     shape = jax.ShapeDtypeStruct
@@ -380,18 +437,17 @@
     ints = lambda *s: shape(s, jnp.int32)
     params = pltpu.CompilerParams(has_side_effects=True, vmem_limit_bytes=40 << 20)
 
-    idx1, lab1, idx2, code2, idx3, lab3, over = pl.pallas_call(
+    idx1, lab1, idx2, code2, idx3, lab3 = pl.pallas_call(
         functools.partial(index_kernel, fronts, rows_n, col_tiles),
         out_shape=(ints(dests), ints(dests, 1, 128), ints(fronts * FEW), ints(fronts, 1, 128),
-                   ints(dests), ints(dests, 1, 128), ints(1)),
+                   ints(dests), ints(dests, 1, 128)),
         in_specs=[smem] * 4,
-        out_specs=(smem,) * 7,
-        scratch_shapes=[pltpu.SMEM((dests,), jnp.int32), pltpu.SMEM((fronts,), jnp.int32)],
+        out_specs=(smem,) * 6,
+        scratch_shapes=[pltpu.SMEM((dests,), jnp.int32), pltpu.SMEM((fronts,), jnp.int32), pltpu.SMEM((1,), jnp.int32)],
         name="index",
     )(child_target[:, 0], child_row, child_col, front_owner)
 
     factor = lax.all_gather(inverse_factor[0], "col", axis=1, tiled=True)
-    over_all = lax.psum(over.astype(jnp.float32), ("front", "row", "col"))
 
     in2, incode, fother, fcols = pl.pallas_call(
         functools.partial(spread_kernel, fronts, rows_n),
@@ -406,39 +462,23 @@
         name="spread",
     )(idx2, code2, child_tiles, front_panel[0])
 
+    block = (rows_dev, cols_dev)
     inc_shape = shape((dests,) + tile_shape, jnp.bfloat16)
+    code_shape = ints(rows_n, fronts, 1, 128)
     send_buf = pltpu.VMEM((dests,) + tile_shape, jnp.bfloat16)
-    first, in_labels, second, in_codes = pl.pallas_call(
+    first, in_labels, second, in_codes, _, over, base, panel_half = pl.pallas_call(
         functools.partial(exchange_kernel, fronts, rows_n, True),
-        out_shape=(inc_shape, ints(dests, 1, 128), inc_shape, ints(rows_n, fronts, 1, 128)),
-        in_specs=[smem, anyspace, vmem, smem, anyspace, vmem],
-        out_specs=(anyspace,) * 4,
-        scratch_shapes=[send_buf, send_buf] + [DMA] * 8 + [DMA((4,))],
-        compiler_params=params,
+        out_shape=(inc_shape, ints(dests, 1, 128), inc_shape, code_shape, code_shape, ints(1, 128),
+                   shape(block, jnp.float32), shape((rows_dev, half), jnp.float32)),
+        in_specs=[smem, anyspace, vmem, smem, anyspace, vmem, smem, vmem, vmem, vmem, vmem, anyspace],
+        out_specs=(hbm, anyspace, hbm, vmem, vmem, vmem, vmem, vmem),
+        scratch_shapes=[send_buf, send_buf, pltpu.VMEM(block, jnp.float32), pltpu.VMEM((rows_dev, 2 * half), jnp.float32)]
+        + [DMA] * 10 + [DMA((5,))],
+        compiler_params=pltpu.CompilerParams(has_side_effects=True, vmem_limit_bytes=46 << 20),
         cost_estimate=pl.CostEstimate(flops=0, bytes_accessed=300_000_000, transcendentals=0),
         name="exchange",
-    )(idx1, lab1, child_tiles, incode, incode, in2)
-
-    live_bound = live_tiles[0] * TILE
-    row_ids = row_place * rows_dev + jnp.arange(rows_dev, dtype=jnp.int32)
-    col_row_ids = col_place * cols_dev + jnp.arange(cols_dev, dtype=jnp.int32)
-
-    def rows_of(left, right, ids):
-        dims = (((1,), (1,)), ((), ()))
-        value = lax.dot_general(left, factor[:, :half], dims, precision=highest, preferred_element_type=jnp.float32)
-        value += lax.dot_general(right, factor[:, half:], dims, precision=highest, preferred_element_type=jnp.float32)
-        return jnp.where(ids[:, None] < live_bound, value, jnp.zeros_like(value))
-
-    mine = front_panel[0]
-    swap = col_place == 1
-    own_panel = rows_of(jnp.where(swap, fother, mine), jnp.where(swap, mine, fother), row_ids)
-    columns = rows_of(fcols[:, 0].reshape(cols_dev, half), fcols[:, 1].reshape(cols_dev, half), col_row_ids)
-    panel_out = lax.dynamic_slice_in_dim(own_panel, col_place * half, half, 1)[None]
-    base = update_block[0] - lax.dot_general(
-        own_panel, columns, (((1,), (1,)), ((), ())), precision=highest, preferred_element_type=jnp.float32
-    )
-
-    block = (rows_dev, cols_dev)
+    )(idx1, lab1, child_tiles, incode, incode, in2, live_tiles, front_panel[0], fother, fcols, factor, update_block[0])
+
     group = dests // rows_n
     whole = pl.BlockSpec(block, lambda i: (0, 0), pipeline_mode=pl.Buffered(1))
     tiles_spec = pl.BlockSpec((group,) + tile_shape, lambda i: (i, 0, 0))
@@ -463,19 +503,20 @@
             name="more",
         )(labels3, value, tiles3)
 
-    base = lax.cond(over_all[0] > 0, further, lambda value: value, base)
-
-    schur_out = pl.pallas_call(
+    base = lax.cond(over[0, FEW] > 0, further, lambda value: value, base)
+
+    panel_spec = pl.BlockSpec((rows_dev // rows_n, half), lambda i: (i, 0))
+    schur_out, panel_out = pl.pallas_call(
         functools.partial(finish_kernel, group, col_tiles, rows_n),
-        out_shape=shape(block, jnp.bfloat16),
+        out_shape=(shape(block, jnp.bfloat16), shape((rows_dev, half), jnp.float32)),
         grid=(rows_n,),
-        in_specs=[smem, smem, smem, whole, tiles_spec, tiles_spec],
-        out_specs=pl.BlockSpec(block, lambda i: (0, 0)),
+        in_specs=[smem, smem, smem, whole, tiles_spec, tiles_spec, panel_spec],
+        out_specs=(pl.BlockSpec(block, lambda i: (0, 0)), panel_spec),
         scratch_shapes=[pltpu.VMEM(block, jnp.float32)],
-        compiler_params=pltpu.CompilerParams(vmem_limit_bytes=40 << 20),
+        compiler_params=pltpu.CompilerParams(vmem_limit_bytes=58 << 20),
         name="finish",
-    )(in_labels, in_codes, live_tiles, base, first, second)[None]
-    return (schur_out, panel_out)
+    )(in_labels, in_codes, live_tiles, base, first, second, panel_half)
+    return (schur_out[None], panel_out[None])
 
 
 def solution(mesh):

time: 459 us -> 248 us (0.54)
  blocking collectives: 81.3 us -> 0 us
  Pallas kernels: 300 us -> 220 us
  matrix products: 43 us -> 0 us
  local copies, waits for them, and re-layouts: 17.1 us -> 10.9 us
    pallas_call x2 -> x0, Pallas kernels: 114 us -> none  [the longest x1 108 us: further(): pl.pallas_call(functools.partial(exchange_kernel, fronts, rows_n, False),...]
    psum x1 -> x0, blocking collectives: 81.3 us -> none  [per_device(): over_all = lax.psum(over.astype(jnp.float32), ('front', 'row', 'col'))]
    dot_general x5 -> x0, matrix products: 43 us -> none  [the longest x2 15.7 us: rows_of(): lax.dot_general(left, factor[:, :half], dims, precision=highest, preferre...]
    pallas_call x1, Pallas kernels: 52.1 us -> 74.9 us  [per_device(): pl.pallas_call(functools.partial(spread_kernel, fronts, rows_n), out_shap...]
    pallas_call x1, Pallas kernels: 116 us -> 124 us  [per_device(): pl.pallas_call(functools.partial(exchange_kernel, fronts, rows_n, True),...]
    unnamed x28 -> x22, local copies, waits for them, and re-layouts: 10.8 us -> 10.3 us
  transfers between devices with their start and end apart: 1 -> 1, of which waited for: 0 -> 0; matrix products, arithmetic and copies ran while one was open for 1% -> 0% of each run, Pallas kernels for 38% -> 34%
where the time goes in v3:
time: 248 us; the launch traced here: 247 us
  Pallas kernels  220 us (89%)
  between operations  15.4 us (6%)
  local copies, waits for them, and re-layouts  10.9 us (4%)
    pallas_call x1, Pallas kernels, per_device(): pl.pallas_call(functools.partial(exchange_kernel, fronts, rows_n, True),...  124 us
    pallas_call x1, Pallas kernels, per_device(): pl.pallas_call(functools.partial(spread_kernel, fronts, rows_n), out_shap...  74.9 us
    pallas_call x1, Pallas kernels, per_device(): pl.pallas_call(functools.partial(finish_kernel, group, col_tiles, rows_n)...  13.3 us
    unnamed x22, local copies, waits for them, and re-layouts  10.3 us
    pallas_call x1, Pallas kernels, per_device(): pl.pallas_call(functools.partial(index_kernel, fronts, rows_n, col_tiles)...  7.89 us
  transfers between devices with their start and end apart: 1, of which 0 were waited for; matrix products, arithmetic and copies ran while one was open for 0% of the time, Pallas kernels for 34%

profile of v3, /device:TPU:1, one launch (start us, length us, event | category | flops | bytes accessed | tf_op | source)
XLA Modules:
  0.0 246.8 jit_solution(8430912659823390376)
XLA Ops:
  7.2 0.0 copy-start.2
  7.2 0.0 all-gather.3.cloned.1.call-start
  7.2 0.7 all-gather.3.cloned.1.call-update
  8.6 7.9 %index.1 = (s32[128]{0:T(128)}, s32[128,1,128]{2,1,0:T(1,128)}, s32[48]{0:T(128)}, s32[16,1,128]{2,1,0:T(1,128)}, s32[128]{0:T(128)S(1)}, /*index=5*/s32[128,1,128]{2,1,0:T(1,128)S(1)}) custom-call(s32[86]{0:T(128)} %bitcast.11, s32[86]{0:T(128)} %crow.1, s32[86]{0:T(128)} %ccol.1, s32[16]{0:T(128)} %owner.1), custom_call_target="tpu_custom_call" | custom-call | tf_op jit(solution)/shard_map/index/pallas_call | solution.py:440
  16.5 0.0 copy-start.1
  16.5 1.1 copy-done.1
  17.6 0.0 copy-start.8
  17.6 0.7 copy-done.8
  18.3 0.0 copy-start.10
  18.3 0.6 copy-done.10
  18.9 74.9 %spread.1 = (bf16[48,128,128]{2,1,0:T(8,128)(2,1)S(1)}, s32[16,1,128]{2,1,0:T(1,128)S(1)}, f32[512,384]{1,0:T(8,128)S(1)}, f32[4,2,512,384]{3,2,1,0:T(8,128)S(1)}) custom-call(s32[48]{0:T(128)S(1)} %copy-done.10, s32[16,1,128]{2,1,0:T(1,128)S(1)} %copy-done.8, bf16[86,128,128]{2,1,0:T(8,128)(2,1)} %refs_2_.1, f32[512,384]{1,0:T(8,128)S(1)} %bitcast.7), custom_call_target="tpu_custom_call" | custom-call | bytes 150000000 | tf_op jit(solution)/shard_map/spread/pallas_call | solution.py:452
  93.8 0.0 copy-start
  93.8 2.7 %copy-done = f32[4,2,512,384]{3,2,1,0:T(8,128)} copy-done((f32[4,2,512,384]{3,2,1,0:T(8,128)}, f32[4,2,512,384]{3,2,1,0:T(8,128)S(1)}, u32[]{:S(2)}) %copy-start) | copy-done | bytes 6291480
  96.5 0.0 copy-done.2
  96.5 1.7 copy-done.3
  98.1 0.8 copy-done.7
  99.0 0.6 copy-done.9
  99.6 123.7 %exchange.1 = (bf16[128,128,128]{2,1,0:T(8,128)(2,1)}, s32[128,1,128]{2,1,0:T(1,128)S(1)}, bf16[128,128,128]{2,1,0:T(8,128)(2,1)}, s32[8,16,1,128]{3,2,1,0:T(1,1...) custom-call(s32[128]{0:T(128)S(1)} %copy-done.9, ...), custom_call_target="tpu_custom_call" | custom-call | bytes 300000000 | tf_op jit(solution)/shard_map/exchange/pallas_call | solution.py:469
  223.3 0.0 copy-start.4
  223.3 0.9 copy-done.4
  224.2 0.6 copy-done.5
  224.8 0.6 copy-done.6
  225.4 0.6 slice.3
  226.7 13.3 %finish.1 = (bf16[512,2048]{1,0:T(8,128)(2,1)}, f32[512,384]{1,0:T(8,128)}) custom-call(s32[128,1,128]{2,1,0:T(1,128)} %copy-done.5, s32[8,16,1,128]{3,2,1,0:T(1,128)} %copy-done.6, s32[1]{0:T(128)S(6)} %copy.14.refs_6_.live, f32[512,2048]{1,0:T(8,128)} %get-tuple-element.58.base, bf16[128,128,128]{2,1,0:T(8,128)(2,1)} %get-tuple-element.53.first, ...), custom_call_target="tpu_custom_call" | custom-call | tf_op jit(solution)/shard_map/finish/pallas_call | solution.py:509
  (7 shorter events, 0.0 us)
Async XLA Ops:
  7.2 89.3 %copy-start.2 = (f32[1,512,384]{2,1,0:T(8,128)S(1)}, f32[1,512,384]{2,1,0:T(8,128)}, u32[]{:S(2)}) copy-start(f32[1,512,384]{2,1,0:T(8,128)} %param.12) | copy-start | bytes 2359300
  7.2 89.3 %all-gather.3.cloned.1.call-start = ((), (), s32[]{:S(2)}) async-start(), calls=%async_computation | async-start | bytes 3538944 | tf_op jit(solution)/shard_map/all_gather | solution.py:450
  16.5 1.1 copy-start.1
  17.6 0.7 copy-start.8
  18.3 0.6 copy-start.10
  93.8 2.7 %copy-start = (f32[4,2,512,384]{3,2,1,0:T(8,128)}, f32[4,2,512,384]{3,2,1,0:T(8,128)S(1)}, u32[]{:S(2)}) copy-start(f32[4,2,512,384]{3,2,1,0:T(8,128)S(1)} %get-tuple-element.46.refs_9_) | copy-start | bytes 18874372
  96.5 1.7 copy-start.3
  98.1 0.8 copy-start.7
  99.0 0.6 copy-start.9
  223.3 0.9 copy-start.4
  224.2 0.6 copy-start.5
  224.8 0.6 copy-start.6
Sparse Core Ops, SparseCore 0:
  9.8 77.0 all-gather.2

commit v4 on v2

v4 whole, which is shorter than its diff:
```python
import functools

import jax
import jax.numpy as jnp
from jax import lax
from jax.experimental import pallas as pl
from jax.experimental.pallas import tpu as pltpu
from jax.sharding import PartitionSpec as P

TILE = 128
FEW = 3
CHUNKS = 4
MESH = pl.DeviceIdType.MESH
DMA = pltpu.SemaphoreType.DMA


def schur_base(live, fown, fother, fcols, wown, wother, update, own_panel, base, panel):
    row, col = lax.axis_index("row"), lax.axis_index("col")
    height, width = base.shape
    half = fown.shape[1]
    step = height // 2
    bound = live[0] * TILE
    mine = pl.ds(pl.multiple_of(col * half, TILE), half)

    def times(a, b):
        return lax.dot_general(
            a, b, (((1,), (1,)), ((), ())), precision=lax.Precision.HIGHEST, preferred_element_type=jnp.float32
        )

    def panel_rows(a, b, start):
        value = times(a, wown[...]) + times(b, wother[...])
        ids = start + lax.broadcasted_iota(jnp.int32, value.shape, 0)
        return jnp.where(ids < bound, value, 0.0)

    @pl.loop(0, 2)
    def _(i):
        rows = pl.ds(pl.multiple_of(i * step, step), step)
        own_panel[rows] = panel_rows(fown[rows], fother[rows], row * height + i * step)

    panel[...] = own_panel[:, mine]

    @pl.loop(0, width // step)
    def _(c):
        rows = pl.ds(pl.multiple_of((c % 2) * step, step), step)
        value = panel_rows(fcols[c // 2, col, rows], fcols[c // 2, 1 - col, rows], col * width + c * step)
        lanes = pl.ds(pl.multiple_of(c * step, step), step)
        base[:, lanes] = update[:, lanes] - times(own_panel[...], value)


def make_tables(fronts, rows_n, col_tiles, target, crow, ccol, owner, codes, picks, idx3, place3):
    dests = fronts * rows_n
    empty = 4 * col_tiles
    bits = rows_n.bit_length() - 1
    amount = target.shape[1]
    t = target[...]
    holder = jnp.zeros_like(t)
    for f in range(fronts):
        holder = jnp.where(lax.shift_right_arithmetic(t, bits) == f, owner[f], holder)
    address = holder * rows_n + (t & (rows_n - 1))
    place = crow[...] * col_tiles + ccol[...]
    grid = (dests, amount)
    i = lax.broadcasted_iota(jnp.int32, grid, 1)
    here = lax.broadcasted_iota(jnp.int32, grid, 0) == address
    wide = (fronts, rows_n, 128)

    def spread(column):
        return jnp.broadcast_to(column, (dests, 128)).reshape(wide)

    first = jnp.min(jnp.where(here, i, amount), axis=1, keepdims=True)
    last = jnp.max(jnp.where(here, i, -1), axis=1, keepdims=True)
    place1 = jnp.sum(jnp.where(i == first, place, 0), axis=1, keepdims=True)
    place2 = jnp.sum(jnp.where(i == last, place, 0), axis=1, keepdims=True)
    place1 = spread(jnp.where(first < amount, place1, empty))
    pick1 = spread(jnp.where(first < amount, first, 0))
    twice = spread(jnp.where(last > first, 1, 0))
    place2, last = spread(place2), spread(last)
    lane = lax.broadcasted_iota(jnp.int32, wide, 2)
    r = lax.broadcasted_iota(jnp.int32, wide, 1)
    rank = jnp.zeros(wide, jnp.int32)
    for q in range(rows_n - 1):
        rank = rank + jnp.where(r > q, twice[:, q : q + 1, :], 0)
    few = jnp.where((rank == lane) & (lane < FEW), twice, 0)
    firsts = lane - 8 == r
    left = jnp.where(rank >= FEW, twice, 0)

    def down(value):
        return jnp.sum(value, axis=1, keepdims=True)

    row_lane = lax.broadcasted_iota(jnp.int32, (fronts, 1, 128), 2)
    over = jnp.sum(down(left), axis=0, keepdims=True)
    code = down(few * (r * empty + place2)) + down(jnp.where(firsts, place1, 0))
    code = jnp.where((row_lane < FEW) & (down(few) == 0), rows_n * empty, code)
    codes[...] = jnp.where(row_lane == FEW, over, code)
    picks[...] = down(few * last) + down(jnp.where(firsts, pick1, 0))
    idx3[...] = (left * last).reshape(dests, 128)
    place3[...] = jnp.where(left > 0, place2, empty).reshape(dests, 128)


def remote(src, dst, ssem, rsem, dev):
    return pltpu.make_async_remote_copy(src, dst, ssem, rsem, device_id=dev, device_id_type=MESH)


def level_kernel(fronts, rows_n, col_tiles, target, crow, ccol, owner, live, tiles_hbm, fown, wown_hbm, update,
                 inc, xin, xcodes, ycodes, over, base, panel, idx3, place3,
                 tiles, send, xsend, send2, in2, codes, picks, incode, pick_s, code_s,
                 fownv, fother, fcols, wown, wother, old, own_panel,
                 ssem, rsem, xssem, xrsem, cssem, crsem, yssem, yrsem, ts, tr, cs, cr, ys, yr, xs, xr, ks, kr, ws, wr, wks, wkr, lsem):
    dests = fronts * rows_n
    empty = 4 * col_tiles
    front, row, col = lax.axis_index("front"), lax.axis_index("row"), lax.axis_index("col")
    me = front * rows_n + row
    x, k = row // 2, row % 2
    j = (x + 4 - 2 * col) % 4
    step_rows = fown.shape[0] // CHUNKS

    def at_j(place):
        return (front, ((place + 2 * col) % 4) * 2 + k, col)

    here = (front, row, col)
    mate = (front, x * 2 + 1 - k, col)
    across = (front, row, 1 - col)

    def part(i):
        return pl.ds(i * step_rows, step_rows)

    def load(n, src, dst):
        return pltpu.make_async_copy(src, dst, lsem.at[n])

    loads = [load(0, tiles_hbm, tiles), load(1, fown, fownv), load(2, wown_hbm, wown), load(3, update, old)]

    @pl.loop(0, CHUNKS)
    def _(i):
        remote(fown.at[part(i)], fother.at[part(i)], ys, yr.at[i], across).start()

    def give(which, half, i, src, dev):
        b = 2 * which + k
        remote(src, fcols.at[b, half, part(i)], xs, xr.at[which, half, i], dev).start()

    def to_mate(which, half, i, src):
        b = 2 * which + k
        remote(src, fcols.at[b, half, part(i)], ks, kr.at[which], mate).start()

    def own_out(half, i, src):
        @pl.when(j == 0)
        def _():
            give(0, half, i, src, at_j(3))
            give(0, half, i, src, at_j(1))
            to_mate(0, half, i, src)

        @pl.when(j == 1)
        def _():
            give(1, half, i, src, at_j(2))
            give(1, half, i, src, at_j(0))
            to_mate(1, half, i, src)

    @pl.loop(0, CHUNKS)
    def _(i):
        own_out(col, i, fown.at[part(i)])

    w_rows = wother.shape[0] // 2
    w_mine = pl.ds(pl.multiple_of(k * w_rows, TILE), w_rows)
    remote(wown_hbm.at[w_mine], wother.at[w_mine], ws, wr, across).start()
    for c in loads:
        c.start()

    make_tables(fronts, rows_n, col_tiles, target, crow, ccol, owner, codes, picks, idx3, place3)
    table = load(4, picks, pick_s)
    table.start()
    table.wait()
    loads[0].wait()

    for t in range(FEW):
        in2[front * FEW + t] = tiles[pick_s[front, 0, t]]
    incode[front] = codes[front]

    @pl.loop(1, fronts)
    def _(s):
        f = jnp.bitwise_xor(front, (s * 7) % fronts)
        for t in range(FEW):
            send2[f * FEW + t] = tiles[pick_s[f, 0, t]]
        dev = (f, row, col)
        remote(send2.at[pl.ds(f * FEW, FEW)], in2.at[pl.ds(front * FEW, FEW)], ts, tr, dev).start()
        remote(codes.at[f], incode.at[front], cs, cr, dev).start()

    send[me] = tiles[pick_s[front, 0, 8 + row]]
    own = load(5, send.at[me], inc.at[me])
    own.start()

    def arrived(which, half, i):
        b = 2 * which + k
        remote(fcols.at[b, half, part(i)], fcols.at[b, half, part(i)], xs, xr.at[which, half, i], mate).wait_recv()

    def pass_on(which, half, i, dev):
        b = 2 * which + k
        src = fcols.at[b, half, part(i)]
        if dev is not None:
            give(which, half, i, src, dev)
        to_mate(which, half, i, src)

    per = dests // (2 * CHUNKS)

    @pl.loop(0, 2 * CHUNKS + 1)
    def _(s):
        @pl.when(s < 2 * CHUNKS)
        def _():
            @pl.loop(0, per)
            def _(inner):
                n = s * per + inner

                @pl.when(n > 0)
                def _():
                    p = jnp.bitwise_xor(me, (n * 37) % dests)
                    f, r = p // rows_n, p % rows_n
                    send[p] = tiles[pick_s[f, 0, 8 + r]]
                    remote(send.at[p], inc.at[me], ssem, rsem, (f, r, col)).start()

            late = s // CHUNKS
            half = (col + late) % 2
            i = s % CHUNKS

            @pl.when(late == 1)
            def _():
                remote(fown.at[part(i)], fother.at[part(i)], ys, yr.at[i], across).wait_recv()
                own_out(half, i, fother.at[part(i)])

            @pl.when(s == CHUNKS)
            def _():
                whalf = remote(wother.at[w_mine], wother.at[w_mine], wks, wr, mate)
                whalf.wait_recv()
                remote(wother.at[w_mine], wother.at[w_mine], wks, wkr, mate).start()

            @pl.when(j == 0)
            def _():
                arrived(1, half, i)
                pass_on(1, half, i, None)

            @pl.when(j == 1)
            def _():
                arrived(0, half, i)
                pass_on(0, half, i, None)

            @pl.when(j == 2)
            def _():
                arrived(1, half, i)
                pass_on(1, half, i, at_j(3))

            @pl.when(j == 3)
            def _():
                arrived(0, half, i)
                pass_on(0, half, i, at_j(2))

        @pl.when(s > 0)
        def _():
            half = (col + (s - 1) // CHUNKS) % 2
            i = (s - 1) % CHUNKS

            @pl.when(j == 2)
            def _():
                arrived(0, half, i)
                pass_on(0, half, i, None)

            @pl.when(j == 3)
            def _():
                arrived(1, half, i)
                pass_on(1, half, i, None)

    some = pl.ds(0, (fronts - 1) * FEW)
    both = remote(send2.at[some], in2.at[some], ts, tr, mate)
    both.wait_send()
    both.wait_recv()
    most = pl.ds(0, fronts - 1)
    got = remote(codes.at[most], incode.at[most], cs, cr, mate)
    got.wait_send()
    got.wait_recv()
    table = load(4, incode, code_s)
    table.start()
    table.wait()

    def pack_row(r):
        @pl.loop(0, fronts)
        def _(g):
            t = 0
            for q in range(1, FEW):
                t = jnp.where(code_s[g, 0, q] // empty == r, q, t)
            xsend[r * fronts + g] = in2[g * FEW + t]

    @pl.loop(0, rows_n)
    def _(s):
        r = jnp.bitwise_xor(row, s)

        @pl.when(s > 0)
        def _():
            pack_row(r)
            dev = (front, r, col)
            remote(xsend.at[pl.ds(r * fronts, fronts)], xin.at[pl.ds(row * fronts, fronts)], xssem, xrsem, dev).start()
            remote(incode, xcodes.at[row], cssem, crsem, dev).start()

        remote(incode, ycodes.at[row], yssem, yrsem, (front, r, 1 - col)).start()

    pack_row(row)
    mine = pl.ds(row * fronts, fronts)
    ownx = load(4, xsend.at[mine], xin.at[mine])
    ownx.start()
    xcodes[row] = incode[...]

    for which in range(2):
        b = 2 * which + 1 - k
        remote(fcols.at[b], fcols.at[b], ks, kr.at[which], mate).wait_recv()
    w_other = pl.ds(pl.multiple_of((1 - k) * w_rows, TILE), w_rows)
    remote(wother.at[w_other], wother.at[w_other], wks, wkr, mate).wait_recv()
    for c in loads[1:]:
        c.wait()

    @pl.when(j < 2)
    def _():
        b = 2 * j + k
        fcols[b, col] = fownv[...]
        fcols[b, 1 - col] = fother[...]

    schur_base(live, fownv, fother, fcols, wown, wother, old, own_panel, base, panel)

    remote(fown, fother, ys, yr.at[0], across).wait_send()
    remote(wother.at[w_mine], wother.at[w_mine], ws, wr, across).wait_send()
    remote(wother.at[w_mine], wother.at[w_mine], wks, wkr, mate).wait_send()
    pairs = fcols.at[pl.ds(0, 2)]
    remote(pairs, pairs, ks, kr.at[0], mate).wait_send()

    @pl.when(j < 2)
    def _():
        remote(pairs, pairs, xs, kr.at[0], mate).wait_send()

    @pl.when(j >= 2)
    def _():
        remote(fcols.at[0], fcols.at[0], xs, kr.at[0], mate).wait_send()

    own.wait()
    ownx.wait()
    some = pl.ds(0, dests - 1)
    both = remote(send.at[some], inc.at[some], ssem, rsem, here)
    both.wait_send()
    both.wait_recv()
    some = pl.ds(0, (rows_n - 1) * fronts)
    both = remote(xsend.at[some], xin.at[some], xssem, xrsem, here)
    both.wait_send()
    both.wait_recv()
    some = pl.ds(0, rows_n - 1)
    both = remote(xcodes.at[some], xcodes.at[some], cssem, crsem, here)
    both.wait_send()
    both.wait_recv()
    both = remote(ycodes, ycodes, yssem, yrsem, here)
    both.wait_send()
    both.wait_recv()
    counts = jnp.sum(xcodes[...] + ycodes[...], axis=0)
    over[...] = jnp.sum(counts, axis=0)


def further_kernel(fronts, rows_n, idx, lab, tiles, inc, inlab, send, ssem, rsem, lssem, lrsem, lsem):
    dests = fronts * rows_n
    front, row, col = lax.axis_index("front"), lax.axis_index("row"), lax.axis_index("col")
    me = front * rows_n + row
    send[me] = tiles[idx[me]]
    own = pltpu.make_async_copy(send.at[me], inc.at[me], lsem.at[0])
    own.start()
    ownlab = pltpu.make_async_copy(lab.at[me], inlab.at[me], lsem.at[1])
    ownlab.start()

    @pl.loop(1, dests)
    def _(n):
        p = jnp.bitwise_xor(me, (n * 37) % dests)
        dev = (p // rows_n, p % rows_n, col)
        send[p] = tiles[idx[p]]
        remote(send.at[p], inc.at[me], ssem, rsem, dev).start()
        remote(lab.at[p], inlab.at[me], lssem, lrsem, dev).start()

    own.wait()
    ownlab.wait()
    some = pl.ds(0, dests - 1)
    both = remote(send.at[some], inc.at[some], ssem, rsem, (front, row, col))
    both.wait_send()
    both.wait_recv()
    labs = remote(lab.at[some], inlab.at[some], lssem, lrsem, (front, row, col))
    labs.wait_send()
    labs.wait_recv()


def add_tile(out, place, col_tiles, tile):
    @pl.when(place < 4 * col_tiles)
    def _():
        r = pl.multiple_of((place // col_tiles) * TILE, TILE)
        c = pl.multiple_of((place % col_tiles) * TILE, TILE)
        out[pl.ds(r, TILE), pl.ds(c, TILE)] += tile[...].astype(jnp.float32)


def more_kernel(group, col_tiles, lab, base, tiles, out):
    step = pl.program_id(0)

    @pl.when(step == 0)
    def _():
        out[...] = base[...]

    @pl.loop(0, group)
    def _(i):
        add_tile(out, lab[step * group + i, 0, 0], col_tiles, tiles.at[i])


def finish_kernel(group, col_tiles, steps, rows_n, code, live, base, first, second, panel_in, out, panel_out, total):
    step = pl.program_id(0)
    row, col = lax.axis_index("row"), lax.axis_index("col")
    empty = 4 * col_tiles

    panel_out[...] = panel_in[...]

    @pl.when(step == 0)
    def _():
        total[...] = base[...]

    @pl.loop(0, group)
    def _(i):
        source = step * group + i
        place = code[source % rows_n, source // rows_n, 0, 8 + row]
        add_tile(total, place, col_tiles, first.at[i])
        place = empty
        for k in range(FEW):
            c = code[step, i, 0, k]
            place = jnp.where(c // empty == row, c % empty, place)
        add_tile(total, place, col_tiles, second.at[i])

    @pl.when(step == steps - 1)
    def _():
        bound = live[0] * TILE
        height, width = total.shape

        @pl.loop(0, height // TILE)
        def _(i):
            rows = pl.ds(pl.multiple_of(i * TILE, TILE), TILE)
            row_ids = row * height + i * TILE + lax.broadcasted_iota(jnp.int32, (TILE, width), 0)
            col_ids = col * width + lax.broadcasted_iota(jnp.int32, (TILE, width), 1)
            inside = (row_ids < bound) & (col_ids < bound)
            out[rows] = jnp.where(inside, total[rows], 0.0).astype(out.dtype)


def per_device(
    update_block,
    front_panel,
    inverse_factor,
    child_tiles,
    child_target,
    child_row,
    child_col,
    front_owner,
    live_tiles,
):
    rows_dev = update_block.shape[1]
    cols_dev = update_block.shape[2]
    fronts = lax.axis_size("front")
    rows_n = lax.axis_size("row")
    dests = fronts * rows_n
    col_tiles = cols_dev // TILE
    half = front_panel.shape[2]

    anyspace = pl.BlockSpec(memory_space=pl.ANY)
    hbm = pl.BlockSpec(memory_space=pltpu.HBM)
    smem = pl.BlockSpec(memory_space=pltpu.SMEM)
    vmem = pl.BlockSpec(memory_space=pltpu.VMEM)
    shape = jax.ShapeDtypeStruct
    tile_shape = (TILE, TILE)
    ints = lambda *s: shape(s, jnp.int32)
    params = pltpu.CompilerParams(has_side_effects=True, vmem_limit_bytes=40 << 20)

    block = (rows_dev, cols_dev)
    group = dests // rows_n
    inc_shape = shape((dests,) + tile_shape, jnp.bfloat16)
    code_shape = ints(rows_n, fronts, 1, 128)
    rows_buf = lambda *n: pltpu.VMEM(n + (rows_dev, half), jnp.float32)
    tiles_buf = lambda n: pltpu.VMEM((n,) + tile_shape, jnp.bfloat16)
    table = lambda space: space((fronts, 1, 128), jnp.int32)
    amount = child_tiles.shape[0]
    first, second, in_codes, _, over, base, panel_half, idx3, place3 = pl.pallas_call(
        functools.partial(level_kernel, fronts, rows_n, col_tiles),
        out_shape=(inc_shape, inc_shape, code_shape, code_shape, ints(1, 128), shape(block, jnp.float32),
                   shape((rows_dev, half), jnp.float32), ints(dests, 128), ints(dests, 128)),
        in_specs=[vmem, vmem, vmem, smem, smem, anyspace, anyspace, anyspace, anyspace],
        out_specs=(hbm, hbm) + (vmem,) * 7,
        scratch_shapes=[
            tiles_buf(amount), tiles_buf(dests), tiles_buf(dests), tiles_buf(fronts * FEW), tiles_buf(fronts * FEW),
            table(pltpu.VMEM), table(pltpu.VMEM), table(pltpu.VMEM), table(pltpu.SMEM), table(pltpu.SMEM),
            rows_buf(), rows_buf(), rows_buf(4, 2),
            pltpu.VMEM((2 * half, half), jnp.float32), pltpu.VMEM((2 * half, half), jnp.float32),
            pltpu.VMEM(block, jnp.float32), pltpu.VMEM((rows_dev, 2 * half), jnp.float32),
        ] + [DMA] * 13 + [DMA((CHUNKS,)), DMA, DMA((2, 2, CHUNKS)), DMA, DMA((2,))] + [DMA] * 4 + [DMA((6,))],
        compiler_params=pltpu.CompilerParams(has_side_effects=True, vmem_limit_bytes=58 << 20),
        cost_estimate=pl.CostEstimate(flops=0, bytes_accessed=300_000_000, transcendentals=0),
        name="level",
    )(child_target.reshape(1, amount), child_row.reshape(1, amount), child_col.reshape(1, amount), front_owner, live_tiles,
      child_tiles, front_panel[0], inverse_factor[0], update_block[0])

    whole = pl.BlockSpec(block, lambda i: (0, 0), pipeline_mode=pl.Buffered(1))
    tiles_spec = pl.BlockSpec((group,) + tile_shape, lambda i: (i, 0, 0))

    def further(value):
        labels = jnp.broadcast_to(place3[:, :1, None], (dests, 1, 128))
        tiles3, labels3 = pl.pallas_call(
            functools.partial(further_kernel, fronts, rows_n),
            out_shape=(inc_shape, ints(dests, 1, 128)),
            in_specs=[smem, anyspace, vmem],
            out_specs=(anyspace,) * 2,
            scratch_shapes=[tiles_buf(dests)] + [DMA] * 4 + [DMA((2,))],
            compiler_params=params,
            name="further",
        )(idx3[:, 0], labels, child_tiles)
        return pl.pallas_call(
            functools.partial(more_kernel, group, col_tiles),
            out_shape=shape(block, jnp.float32),
            grid=(rows_n,),
            in_specs=[smem, whole, tiles_spec],
            out_specs=pl.BlockSpec(block, lambda i: (0, 0)),
            compiler_params=pltpu.CompilerParams(vmem_limit_bytes=40 << 20),
            name="more",
        )(labels3, value, tiles3)

    base = lax.cond(over[0, FEW] > 0, further, lambda value: value, base)

    panel_spec = pl.BlockSpec((rows_dev // rows_n, half), lambda i: (i, 0))
    schur_out, panel_out = pl.pallas_call(
        functools.partial(finish_kernel, group, col_tiles, rows_n, rows_n),
        out_shape=(shape(block, jnp.bfloat16), shape((rows_dev, half), jnp.float32)),
        grid=(rows_n,),
        in_specs=[smem, smem, whole, tiles_spec, tiles_spec, panel_spec],
        out_specs=(pl.BlockSpec(block, lambda i: (0, 0)), panel_spec),
        scratch_shapes=[pltpu.VMEM(block, jnp.float32)],
        compiler_params=pltpu.CompilerParams(vmem_limit_bytes=58 << 20),
        name="finish",
    )(in_codes, live_tiles, base, first, second, panel_half)
    return (schur_out[None], panel_out[None])


def solution(mesh):
    return jax.shard_map(
        per_device,
        mesh=mesh,
        in_specs=(
            P("front", "row", "col"),
            P("front", "row", "col"),
            P("front", None, "col"),
            P(("front", "row", "col"), None, None),
            P(("front", "row", "col"), None),
            P(("front", "row", "col")),
            P(("front", "row", "col")),
            P(),
            P("front"),
        ),
        out_specs=(P("front", "row", "col"), P("front", "row", "col")),
        check_vma=False,
    )
```

time: 459 us -> 196 us (0.43)
  Pallas kernels: 300 us -> 192 us
  blocking collectives: 81.3 us -> 0 us
  matrix products: 43 us -> 0 us
  local copies, waits for them, and re-layouts: 17.1 us -> 1.16 us
  between operations: 16.1 us -> 1.97 us
    pallas_call x6 -> x2, Pallas kernels: 300 us -> 192 us  [the longest x1 178 us: per_device(): pl.pallas_call(functools.partial(level_kernel, fronts, rows_n, col_tiles)...]
    psum x1 -> x0, blocking collectives: 81.3 us -> none  [per_device(): over_all = lax.psum(over.astype(jnp.float32), ('front', 'row', 'col'))]
    dot_general x5 -> x0, matrix products: 43 us -> none  [the longest x2 15.7 us: rows_of(): lax.dot_general(left, factor[:, :half], dims, precision=highest, preferre...]
    unnamed x28 -> x2, local copies, waits for them, and re-layouts: 10.8 us -> 0.01 us
  transfers between devices with their start and end apart: 1 -> 0, of which waited for: 0 -> 0; matrix products, arithmetic and copies ran while one was open for 1% -> 0% of each run, Pallas kernels for 38% -> 0%
where the time goes in v4:
time: 196 us; the launch traced here: 195 us
  Pallas kernels  192 us (98%)
  between operations  1.97 us (1%)
    pallas_call x1, Pallas kernels, per_device(): pl.pallas_call(functools.partial(level_kernel, fronts, rows_n, col_tiles)...  178 us
    pallas_call x1, Pallas kernels, per_device(): pl.pallas_call(functools.partial(finish_kernel, group, col_tiles, rows_n,...  13.7 us

profile of v4, /device:TPU:1, one launch (start us, length us, event | category | flops | bytes accessed | tf_op | source)
XLA Modules:
  0.0 194.7 jit_solution(11910063140369280)
XLA Ops:
  1.3 0.0 copy-start.1
  1.3 177.9 %level.1 = (bf16[128,128,128]{2,1,0:T(8,128)(2,1)}, bf16[128,128,128]{2,1,0:T(8,128)(2,1)}, s32[8,16,1,128]{3,2,1,0:T(1,128)}, s32[8,16,1,128]{3,2,1,0:T(1,128)}...) custom-call(s32[1,86]{1,0:T(1,128)} %bitcast.16, ...), custom_call_target="tpu_custom_call" | custom-call | bytes 300000000 | tf_op jit(solution)/shard_map/level/pallas_call | solution.py:478
  179.2 1.2 slice.9
  181.0 0.0 copy-done.1
  181.0 13.7 %finish.1 = (bf16[512,2048]{1,0:T(8,128)(2,1)}, f32[512,384]{1,0:T(8,128)}) custom-call(s32[8,16,1,128]{3,2,1,0:T(1,128)} %get-tuple-element.30.code, s32[1]{0:T(128)S(6)} %copy.16.live, f32[512,2048]{1,0:T(8,128)} %get-tuple-element.44.base, bf16[128,128,128]{2,1,0:T(8,128)(2,1)} %get-tuple-element.35.first, ...), custom_call_target="tpu_custom_call" | custom-call | tf_op jit(solution)/shard_map/finish/pallas_call | solution.py:524
  (1 shorter events, 0.0 us)
Async XLA Ops:
  1.3 179.7 %copy-start.1 = (bf16[86,128,128]{2,1,0:T(8,128)(2,1)S(1)}, bf16[86,128,128]{2,1,0:T(8,128)(2,1)}, u32[]{:S(2)}) copy-start(bf16[86,128,128]{2,1,0:T(8,128)(2,1)} %tiles_hbm.1) | copy-start | bytes 8454148

commit v5 on v4

--- a/solution.py
+++ b/solution.py
@@ -9,14 +9,15 @@
 
 TILE = 128
 FEW = 3
-CHUNKS = 4
+EARLY = 72
+CHUNKS = 2
 MESH = pl.DeviceIdType.MESH
 DMA = pltpu.SemaphoreType.DMA
 
 
-def schur_base(live, fown, fother, fcols, wown, wother, update, own_panel, base, panel):
+def schur_base(live, fown, fother, fcols, wown, wother, update, own_panel, panel):
     row, col = lax.axis_index("row"), lax.axis_index("col")
-    height, width = base.shape
+    height, width = update.shape
     half = fown.shape[1]
     step = height // 2
     bound = live[0] * TILE
@@ -44,7 +45,7 @@
         rows = pl.ds(pl.multiple_of((c % 2) * step, step), step)
         value = panel_rows(fcols[c // 2, col, rows], fcols[c // 2, 1 - col, rows], col * width + c * step)
         lanes = pl.ds(pl.multiple_of(c * step, step), step)
-        base[:, lanes] = update[:, lanes] - times(own_panel[...], value)
+        update[:, lanes] = update[:, lanes] - times(own_panel[...], value)
 
 
 def make_tables(fronts, rows_n, col_tiles, target, crow, ccol, owner, codes, picks, idx3, place3):
@@ -101,15 +102,16 @@
 
 
 def level_kernel(fronts, rows_n, col_tiles, target, crow, ccol, owner, live, tiles_hbm, fown, wown_hbm, update,
-                 inc, xin, xcodes, ycodes, over, base, panel, idx3, place3,
+                 inc, xin, places, over, base, panel, idx3, place3,
                  tiles, send, xsend, send2, in2, codes, picks, incode, pick_s, code_s,
-                 fownv, fother, fcols, wown, wother, old, own_panel,
+                 fownv, fother, fcols, wown, wother, old, own_panel, half_panel, xcodes, ycodes,
                  ssem, rsem, xssem, xrsem, cssem, crsem, yssem, yrsem, ts, tr, cs, cr, ys, yr, xs, xr, ks, kr, ws, wr, wks, wkr, lsem):
     dests = fronts * rows_n
     empty = 4 * col_tiles
     front, row, col = lax.axis_index("front"), lax.axis_index("row"), lax.axis_index("col")
     me = front * rows_n + row
     x, k = row // 2, row % 2
+    place_bits = empty.bit_length() - 1
     j = (x + 4 - 2 * col) % 4
     step_rows = fown.shape[0] // CHUNKS
 
@@ -197,7 +199,13 @@
             give(which, half, i, src, dev)
         to_mate(which, half, i, src)
 
-    per = dests // (2 * CHUNKS)
+    def straight(n):
+        p = jnp.bitwise_xor(me, (n * 37) % dests)
+        f, r = p // rows_n, p % rows_n
+        send[p] = tiles[pick_s[f, 0, 8 + r]]
+        remote(send.at[p], inc.at[me], ssem, rsem, (f, r, col)).start()
+
+    per = EARLY // (2 * CHUNKS)
 
     @pl.loop(0, 2 * CHUNKS + 1)
     def _(s):
@@ -209,10 +217,7 @@
 
                 @pl.when(n > 0)
                 def _():
-                    p = jnp.bitwise_xor(me, (n * 37) % dests)
-                    f, r = p // rows_n, p % rows_n
-                    send[p] = tiles[pick_s[f, 0, 8 + r]]
-                    remote(send.at[p], inc.at[me], ssem, rsem, (f, r, col)).start()
+                    straight(n)
 
             late = s // CHUNKS
             half = (col + late) % 2
@@ -276,13 +281,11 @@
     table.start()
     table.wait()
 
-    def pack_row(r):
-        @pl.loop(0, fronts)
-        def _(g):
-            t = 0
-            for q in range(1, FEW):
-                t = jnp.where(code_s[g, 0, q] // empty == r, q, t)
-            xsend[r * fronts + g] = in2[g * FEW + t]
+    def pack_one(r, g):
+        t = 0
+        for q in range(1, FEW):
+            t = jnp.where(lax.shift_right_logical(code_s[g, 0, q], place_bits) == r, q, t)
+        xsend[r * fronts + g] = in2[g * FEW + t]
 
     @pl.loop(0, rows_n)
     def _(s):
@@ -290,14 +293,31 @@
 
         @pl.when(s > 0)
         def _():
-            pack_row(r)
-            dev = (front, r, col)
-            remote(xsend.at[pl.ds(r * fronts, fronts)], xin.at[pl.ds(row * fronts, fronts)], xssem, xrsem, dev).start()
-            remote(incode, xcodes.at[row], cssem, crsem, dev).start()
+            remote(incode, xcodes.at[row], cssem, crsem, (front, r, col)).start()
 
         remote(incode, ycodes.at[row], yssem, yrsem, (front, r, 1 - col)).start()
 
-    pack_row(row)
+    then = (dests - EARLY) // (rows_n - 1)
+
+    @pl.loop(1, rows_n)
+    def _(s):
+        r = jnp.bitwise_xor(row, s)
+
+        @pl.loop(0, fronts)
+        def _(g):
+            pack_one(r, g)
+
+        src = xsend.at[pl.ds(r * fronts, fronts)]
+        remote(src, xin.at[pl.ds(row * fronts, fronts)], xssem, xrsem, (front, r, col)).start()
+
+        @pl.loop(0, then)
+        def _(q):
+            straight(EARLY + (s - 1) * then + q)
+
+    @pl.loop(0, fronts)
+    def _(g):
+        pack_one(row, g)
+
     mine = pl.ds(row * fronts, fronts)
     ownx = load(4, xsend.at[mine], xin.at[mine])
     ownx.start()
@@ -317,7 +337,30 @@
         fcols[b, col] = fownv[...]
         fcols[b, 1 - col] = fother[...]
 
-    schur_base(live, fownv, fother, fcols, wown, wother, old, own_panel, base, panel)
+    schur_base(live, fownv, fother, fcols, wown, wother, old, own_panel, half_panel)
+    results = [load(1, old, base), load(2, half_panel, panel)]
+    for c in results:
+        c.start()
+
+
+    some = pl.ds(0, rows_n - 1)
+    both = remote(xcodes.at[some], xcodes.at[some], cssem, crsem, here)
+    both.wait_send()
+    both.wait_recv()
+    both = remote(ycodes, ycodes, yssem, yrsem, here)
+    both.wait_send()
+    both.wait_recv()
+    lane = lax.broadcasted_iota(jnp.int32, (fronts, 1, 128), 2)
+    slot = lax.broadcasted_iota(jnp.int32, (fronts, 1, 128), 0)
+    left = jnp.zeros((fronts, 1, 128), jnp.int32)
+    for r in range(rows_n):
+        code = xcodes[r]
+        left = left + code + ycodes[r]
+        one = jnp.sum(jnp.where(lane == 8 + row, code, 0), axis=2, keepdims=True)
+        match = (lane < FEW) & (lax.shift_right_logical(code, place_bits) == row)
+        two = jnp.min(jnp.where(match, code & (empty - 1), empty), axis=2, keepdims=True)
+        places[r] = jnp.sum(jnp.where(lane == slot, one, 0) + jnp.where(lane == slot + fronts, two, 0), axis=0)
+    over[0] = jnp.sum(jnp.where(lane == FEW, left, 0))
 
     remote(fown, fother, ys, yr.at[0], across).wait_send()
     remote(wother.at[w_mine], wother.at[w_mine], ws, wr, across).wait_send()
@@ -335,6 +378,8 @@
 
     own.wait()
     ownx.wait()
+    for c in results:
+        c.wait()
     some = pl.ds(0, dests - 1)
     both = remote(send.at[some], inc.at[some], ssem, rsem, here)
     both.wait_send()
@@ -343,15 +388,6 @@
     both = remote(xsend.at[some], xin.at[some], xssem, xrsem, here)
     both.wait_send()
     both.wait_recv()
-    some = pl.ds(0, rows_n - 1)
-    both = remote(xcodes.at[some], xcodes.at[some], cssem, crsem, here)
-    both.wait_send()
-    both.wait_recv()
-    both = remote(ycodes, ycodes, yssem, yrsem, here)
-    both.wait_send()
-    both.wait_recv()
-    counts = jnp.sum(xcodes[...] + ycodes[...], axis=0)
-    over[...] = jnp.sum(counts, axis=0)
 
 
 def further_kernel(fronts, rows_n, idx, lab, tiles, inc, inlab, send, ssem, rsem, lssem, lrsem, lsem):
@@ -403,40 +439,52 @@
         add_tile(out, lab[step * group + i, 0, 0], col_tiles, tiles.at[i])
 
 
-def finish_kernel(group, col_tiles, steps, rows_n, code, live, base, first, second, panel_in, out, panel_out, total):
-    step = pl.program_id(0)
+def finish_kernel(fronts, rows_n, col_tiles, places, live, base, first, second, panel, out, panel_out,
+                  fbuf, sbuf, total, obuf, fsem, ssem, osem, psem, bsem):
     row, col = lax.axis_index("row"), lax.axis_index("col")
-    empty = 4 * col_tiles
-
-    panel_out[...] = panel_in[...]
-
-    @pl.when(step == 0)
-    def _():
-        total[...] = base[...]
-
-    @pl.loop(0, group)
+    bound = live[0] * TILE
+    height, width = total.shape
+    copy = pltpu.make_async_copy
+
+    def tiles_of(r):
+        part = pl.ds(r * fronts, fronts)
+        return copy(first.at[part], fbuf.at[part], fsem.at[r]), copy(second.at[part], sbuf.at[part], ssem.at[r])
+
+    fill = copy(base, total, bsem)
+    fill.start()
+    for r in range(rows_n):
+        for c in tiles_of(r):
+            c.start()
+    copy(panel, panel_out, psem).start()
+    fill.wait()
+
+    @pl.loop(0, rows_n)
+    def _(s):
+        for c in tiles_of(s):
+            c.wait()
+        for i in range(fronts):
+            front = s * (fronts // rows_n) + i // rows_n
+            add_tile(total, places[i % rows_n, 0, front], col_tiles, fbuf.at[s * fronts + i])
+            add_tile(total, places[s, 0, fronts + i], col_tiles, sbuf.at[s * fronts + i])
+
+    def rows_out(i):
+        rows = pl.ds(pl.multiple_of(i * TILE, TILE), TILE)
+        return copy(obuf.at[rows], out.at[rows], osem.at[i])
+
+    @pl.loop(0, height // TILE)
     def _(i):
-        source = step * group + i
-        place = code[source % rows_n, source // rows_n, 0, 8 + row]
-        add_tile(total, place, col_tiles, first.at[i])
-        place = empty
-        for k in range(FEW):
-            c = code[step, i, 0, k]
-            place = jnp.where(c // empty == row, c % empty, place)
-        add_tile(total, place, col_tiles, second.at[i])
-
-    @pl.when(step == steps - 1)
-    def _():
-        bound = live[0] * TILE
-        height, width = total.shape
-
-        @pl.loop(0, height // TILE)
-        def _(i):
-            rows = pl.ds(pl.multiple_of(i * TILE, TILE), TILE)
-            row_ids = row * height + i * TILE + lax.broadcasted_iota(jnp.int32, (TILE, width), 0)
-            col_ids = col * width + lax.broadcasted_iota(jnp.int32, (TILE, width), 1)
-            inside = (row_ids < bound) & (col_ids < bound)
-            out[rows] = jnp.where(inside, total[rows], 0.0).astype(out.dtype)
+        rows = pl.ds(pl.multiple_of(i * TILE, TILE), TILE)
+        row_ids = row * height + i * TILE + lax.broadcasted_iota(jnp.int32, (TILE, 1), 0)
+        col_ids = col * width + lax.broadcasted_iota(jnp.int32, (1, width), 1)
+        inside = (row_ids < bound) & (col_ids < bound)
+        obuf[rows] = jnp.where(inside, total[rows], 0.0).astype(obuf.dtype)
+        rows_out(i).start()
+
+    @pl.loop(0, height // TILE)
+    def _(i):
+        rows_out(i).wait()
+
+    copy(panel, panel_out, psem).wait()
 
 
 def per_device(
@@ -470,23 +518,23 @@
     block = (rows_dev, cols_dev)
     group = dests // rows_n
     inc_shape = shape((dests,) + tile_shape, jnp.bfloat16)
-    code_shape = ints(rows_n, fronts, 1, 128)
     rows_buf = lambda *n: pltpu.VMEM(n + (rows_dev, half), jnp.float32)
     tiles_buf = lambda n: pltpu.VMEM((n,) + tile_shape, jnp.bfloat16)
     table = lambda space: space((fronts, 1, 128), jnp.int32)
     amount = child_tiles.shape[0]
-    first, second, in_codes, _, over, base, panel_half, idx3, place3 = pl.pallas_call(
+    first, second, places, over, base, panel_half, idx3, place3 = pl.pallas_call(
         functools.partial(level_kernel, fronts, rows_n, col_tiles),
-        out_shape=(inc_shape, inc_shape, code_shape, code_shape, ints(1, 128), shape(block, jnp.float32),
+        out_shape=(inc_shape, inc_shape, ints(rows_n, 1, 128), ints(1), shape(block, jnp.float32),
                    shape((rows_dev, half), jnp.float32), ints(dests, 128), ints(dests, 128)),
         in_specs=[vmem, vmem, vmem, smem, smem, anyspace, anyspace, anyspace, anyspace],
-        out_specs=(hbm, hbm) + (vmem,) * 7,
+        out_specs=(hbm, hbm, vmem, smem, hbm, hbm, vmem, vmem),
         scratch_shapes=[
             tiles_buf(amount), tiles_buf(dests), tiles_buf(dests), tiles_buf(fronts * FEW), tiles_buf(fronts * FEW),
             table(pltpu.VMEM), table(pltpu.VMEM), table(pltpu.VMEM), table(pltpu.SMEM), table(pltpu.SMEM),
             rows_buf(), rows_buf(), rows_buf(4, 2),
             pltpu.VMEM((2 * half, half), jnp.float32), pltpu.VMEM((2 * half, half), jnp.float32),
-            pltpu.VMEM(block, jnp.float32), pltpu.VMEM((rows_dev, 2 * half), jnp.float32),
+            pltpu.VMEM(block, jnp.float32), pltpu.VMEM((rows_dev, 2 * half), jnp.float32), rows_buf(),
+            pltpu.VMEM((rows_n, fronts, 1, 128), jnp.int32), pltpu.VMEM((rows_n, fronts, 1, 128), jnp.int32),
         ] + [DMA] * 13 + [DMA((CHUNKS,)), DMA, DMA((2, 2, CHUNKS)), DMA, DMA((2,))] + [DMA] * 4 + [DMA((6,))],
         compiler_params=pltpu.CompilerParams(has_side_effects=True, vmem_limit_bytes=58 << 20),
         cost_estimate=pl.CostEstimate(flops=0, bytes_accessed=300_000_000, transcendentals=0),
@@ -518,19 +566,20 @@
             name="more",
         )(labels3, value, tiles3)
 
-    base = lax.cond(over[0, FEW] > 0, further, lambda value: value, base)
-
-    panel_spec = pl.BlockSpec((rows_dev // rows_n, half), lambda i: (i, 0))
+    base = lax.cond(over[0] > 0, further, lambda value: value, base)
+
     schur_out, panel_out = pl.pallas_call(
-        functools.partial(finish_kernel, group, col_tiles, rows_n, rows_n),
+        functools.partial(finish_kernel, fronts, rows_n, col_tiles),
         out_shape=(shape(block, jnp.bfloat16), shape((rows_dev, half), jnp.float32)),
-        grid=(rows_n,),
-        in_specs=[smem, smem, whole, tiles_spec, tiles_spec, panel_spec],
-        out_specs=(pl.BlockSpec(block, lambda i: (0, 0)), panel_spec),
-        scratch_shapes=[pltpu.VMEM(block, jnp.float32)],
+        in_specs=[smem, smem, hbm, hbm, hbm, vmem],
+        out_specs=(hbm, hbm),
+        scratch_shapes=[
+            tiles_buf(dests), tiles_buf(dests), pltpu.VMEM(block, jnp.float32), pltpu.VMEM(block, jnp.bfloat16),
+            DMA((rows_n,)), DMA((rows_n,)), DMA((rows_dev // TILE,)), DMA, DMA,
+        ],
         compiler_params=pltpu.CompilerParams(vmem_limit_bytes=58 << 20),
         name="finish",
-    )(in_codes, live_tiles, base, first, second, panel_half)
+    )(places, live_tiles, base, first, second, panel_half)
     return (schur_out[None], panel_out[None])
 
 

time: 196 us -> 190 us (0.969)
  Pallas kernels: 192 us -> 186 us
    pallas_call x1, Pallas kernels: 178 us -> 175 us  [per_device(): pl.pallas_call(functools.partial(level_kernel, fronts, rows_n, col_tiles)...]
    pallas_call x1, Pallas kernels: 13.7 us -> 10.9 us  [per_device(): pl.pallas_call(functools.partial(finish_kernel, fronts, rows_n, col_tiles...]
where the time goes in v5:
time: 190 us; the launch traced here: 188 us
  Pallas kernels  186 us (98%)
  between operations  1.99 us (1%)
    pallas_call x1, Pallas kernels, per_device(): pl.pallas_call(functools.partial(level_kernel, fronts, rows_n, col_tiles)...  175 us
    pallas_call x1, Pallas kernels, per_device(): pl.pallas_call(functools.partial(finish_kernel, fronts, rows_n, col_tiles...  10.9 us

profile of v5, /device:TPU:1, one launch (start us, length us, event | category | flops | bytes accessed | tf_op | source)
XLA Modules:
  0.0 187.8 jit_solution(18372368918929458526)
XLA Ops:
  1.3 0.0 copy-start.1
  1.3 174.9 %level.1 = (bf16[128,128,128]{2,1,0:T(8,128)(2,1)}, bf16[128,128,128]{2,1,0:T(8,128)(2,1)}, s32[8,1,128]{2,1,0:T(1,128)}, s32[1]{0:T(128)}, f32[512,2048]{1,0:T(...) custom-call(s32[1,86]{1,0:T(1,128)} %bitcast.16, s32[1,86]{1,0:T(1,128)} %bitcast.17, ...), custom_call_target="tpu_custom_call" | custom-call | bytes 300000000 | tf_op jit(solution)/shard_map/level/pallas_call | solution.py:525
  176.9 0.0 copy-done.1
  176.9 10.9 %finish.1 = (bf16[512,2048]{1,0:T(8,128)(2,1)}, f32[512,384]{1,0:T(8,128)}) custom-call(s32[8,1,128]{2,1,0:T(1,128)} %get-tuple-element.30.places, s32[1]{0:T(128)S(6)} %copy.16.live, f32[512,2048]{1,0:T(8,128)} %get-tuple-element.44.base, bf16[128,128,128]{2,1,0:T(8,128)(2,1)} %get-tuple-element.35.first, bf16[128,128,128]{2,1,0:T(8,128)(2,1)} %get-tuple-element.36.second, ...), custom_call_target="tpu_custom_call" | custom-call | tf_op jit(solution)/shard_map/finish/pallas_call | solution.py:571
  (1 shorter events, 0.0 us)
Async XLA Ops:
  1.3 175.6 %copy-start.1 = (bf16[86,128,128]{2,1,0:T(8,128)(2,1)S(1)}, bf16[86,128,128]{2,1,0:T(8,128)(2,1)}, u32[]{:S(2)}) copy-start(bf16[86,128,128]{2,1,0:T(8,128)(2,1)} %tiles_hbm.1) | copy-start | bytes 8454148

commit v6 on v5

--- a/solution.py
+++ b/solution.py
@@ -440,7 +440,7 @@
 
 
 def finish_kernel(fronts, rows_n, col_tiles, places, live, base, first, second, panel, out, panel_out,
-                  fbuf, sbuf, total, obuf, fsem, ssem, osem, psem, bsem):
+                  fbuf, sbuf, total, old, obuf, fsem, ssem, osem, psem, bsem):
     row, col = lax.axis_index("row"), lax.axis_index("col")
     bound = live[0] * TILE
     height, width = total.shape
@@ -450,13 +450,13 @@
         part = pl.ds(r * fronts, fronts)
         return copy(first.at[part], fbuf.at[part], fsem.at[r]), copy(second.at[part], sbuf.at[part], ssem.at[r])
 
-    fill = copy(base, total, bsem)
-    fill.start()
     for r in range(rows_n):
         for c in tiles_of(r):
             c.start()
+    fill = copy(base, old, bsem)
+    fill.start()
     copy(panel, panel_out, psem).start()
-    fill.wait()
+    total[...] = jnp.zeros_like(total)
 
     @pl.loop(0, rows_n)
     def _(s):
@@ -467,6 +467,8 @@
             add_tile(total, places[i % rows_n, 0, front], col_tiles, fbuf.at[s * fronts + i])
             add_tile(total, places[s, 0, fronts + i], col_tiles, sbuf.at[s * fronts + i])
 
+    fill.wait()
+
     def rows_out(i):
         rows = pl.ds(pl.multiple_of(i * TILE, TILE), TILE)
         return copy(obuf.at[rows], out.at[rows], osem.at[i])
@@ -477,7 +479,7 @@
         row_ids = row * height + i * TILE + lax.broadcasted_iota(jnp.int32, (TILE, 1), 0)
         col_ids = col * width + lax.broadcasted_iota(jnp.int32, (1, width), 1)
         inside = (row_ids < bound) & (col_ids < bound)
-        obuf[rows] = jnp.where(inside, total[rows], 0.0).astype(obuf.dtype)
+        obuf[rows] = jnp.where(inside, old[rows] + total[rows], 0.0).astype(obuf.dtype)
         rows_out(i).start()
 
     @pl.loop(0, height // TILE)
@@ -574,7 +576,8 @@
         in_specs=[smem, smem, hbm, hbm, hbm, vmem],
         out_specs=(hbm, hbm),
         scratch_shapes=[
-            tiles_buf(dests), tiles_buf(dests), pltpu.VMEM(block, jnp.float32), pltpu.VMEM(block, jnp.bfloat16),
+            tiles_buf(dests), tiles_buf(dests), pltpu.VMEM(block, jnp.float32), pltpu.VMEM(block, jnp.float32),
+            pltpu.VMEM(block, jnp.bfloat16),
             DMA((rows_n,)), DMA((rows_n,)), DMA((rows_dev // TILE,)), DMA, DMA,
         ],
         compiler_params=pltpu.CompilerParams(vmem_limit_bytes=58 << 20),

time: 190 us -> 187 us (0.984)
  Pallas kernels: 186 us -> 183 us
    pallas_call x1, Pallas kernels: 10.9 us -> 7.77 us  [per_device(): pl.pallas_call(functools.partial(finish_kernel, fronts, rows_n, col_tiles...]
where the time goes in v6:
time: 187 us; the launch traced here: 185 us
  Pallas kernels  183 us (98%)
  between operations  1.99 us (1%)
    pallas_call x1, Pallas kernels, per_device(): pl.pallas_call(functools.partial(level_kernel, fronts, rows_n, col_tiles)...  175 us
    pallas_call x1, Pallas kernels, per_device(): pl.pallas_call(functools.partial(finish_kernel, fronts, rows_n, col_tiles...  7.77 us

profile of v6, /device:TPU:1, one launch (start us, length us, event | category | flops | bytes accessed | tf_op | source)
XLA Modules:
  0.0 184.7 jit_solution(9585138944599513020)
XLA Ops:
  1.3 0.0 copy-start.1
  1.3 174.9 %level.1 = (bf16[128,128,128]{2,1,0:T(8,128)(2,1)}, bf16[128,128,128]{2,1,0:T(8,128)(2,1)}, s32[8,1,128]{2,1,0:T(1,128)}, s32[1]{0:T(128)}, f32[512,2048]{1,0:T(...) custom-call(s32[1,86]{1,0:T(1,128)} %bitcast.16, s32[1,86]{1,0:T(1,128)} %bitcast.17, ...), custom_call_target="tpu_custom_call" | custom-call | bytes 300000000 | tf_op jit(solution)/shard_map/level/pallas_call | solution.py:527
  176.9 0.0 copy-done.1
  176.9 7.8 %finish.1 = (bf16[512,2048]{1,0:T(8,128)(2,1)}, f32[512,384]{1,0:T(8,128)}) custom-call(s32[8,1,128]{2,1,0:T(1,128)} %get-tuple-element.30.places, s32[1]{0:T(128)S(6)} %copy.16.live, f32[512,2048]{1,0:T(8,128)} %get-tuple-element.44.base, bf16[128,128,128]{2,1,0:T(8,128)(2,1)} %get-tuple-element.35.first, bf16[128,128,128]{2,1,0:T(8,128)(2,1)} %get-tuple-element.36.second, ...), custom_call_target="tpu_custom_call" | custom-call | tf_op jit(solution)/shard_map/finish/pallas_call | solution.py:573
  (1 shorter events, 0.0 us)
Async XLA Ops:
  1.3 175.6 %copy-start.1 = (bf16[86,128,128]{2,1,0:T(8,128)(2,1)S(1)}, bf16[86,128,128]{2,1,0:T(8,128)(2,1)}, u32[]{:S(2)}) copy-start(bf16[86,128,128]{2,1,0:T(8,128)(2,1)} %tiles_hbm.1) | copy-start | bytes 8454148

commit v7 on v6

--- a/solution.py
+++ b/solution.py
@@ -9,8 +9,8 @@
 
 TILE = 128
 FEW = 3
-EARLY = 72
-CHUNKS = 2
+EARLY = 100
+CHUNKS = 1
 MESH = pl.DeviceIdType.MESH
 DMA = pltpu.SemaphoreType.DMA
 

time: 187 us -> 185 us (0.989)
  no operation moved by 1% of the time
where the time goes in v7:
time: 185 us; the launch traced here: 184 us
  Pallas kernels  182 us (98%)
  between operations  1.99 us (1%)
    pallas_call x1, Pallas kernels, per_device(): pl.pallas_call(functools.partial(level_kernel, fronts, rows_n, col_tiles)...  174 us
    pallas_call x1, Pallas kernels, per_device(): pl.pallas_call(functools.partial(finish_kernel, fronts, rows_n, col_tiles...  7.79 us

profile of v7, /device:TPU:1, one launch (start us, length us, event | category | flops | bytes accessed | tf_op | source)
XLA Modules:
  0.0 183.6 jit_solution(5955767135167669860)
XLA Ops:
  1.3 0.0 copy-start.1
  1.3 173.8 %level.1 = (bf16[128,128,128]{2,1,0:T(8,128)(2,1)}, bf16[128,128,128]{2,1,0:T(8,128)(2,1)}, s32[8,1,128]{2,1,0:T(1,128)}, s32[1]{0:T(128)}, f32[512,2048]{1,0:T(...) custom-call(s32[1,86]{1,0:T(1,128)} %bitcast.16, s32[1,86]{1,0:T(1,128)} %bitcast.17, ...), custom_call_target="tpu_custom_call" | custom-call | bytes 300000000 | tf_op jit(solution)/shard_map/level/pallas_call | solution.py:527
  175.8 0.0 copy-done.1
  175.8 7.8 %finish.1 = (bf16[512,2048]{1,0:T(8,128)(2,1)}, f32[512,384]{1,0:T(8,128)}) custom-call(s32[8,1,128]{2,1,0:T(1,128)} %get-tuple-element.30.places, s32[1]{0:T(128)S(6)} %copy.16.live, f32[512,2048]{1,0:T(8,128)} %get-tuple-element.44.base, bf16[128,128,128]{2,1,0:T(8,128)(2,1)} %get-tuple-element.35.first, bf16[128,128,128]{2,1,0:T(8,128)(2,1)} %get-tuple-element.36.second, ...), custom_call_target="tpu_custom_call" | custom-call | tf_op jit(solution)/shard_map/finish/pallas_call | solution.py:573
  (1 shorter events, 0.0 us)
Async XLA Ops:
  1.3 174.5 %copy-start.1 = (bf16[86,128,128]{2,1,0:T(8,128)(2,1)S(1)}, bf16[86,128,128]{2,1,0:T(8,128)(2,1)}, u32[]{:S(2)}) copy-start(bf16[86,128,128]{2,1,0:T(8,128)(2,1)} %tiles_hbm.1) | copy-start | bytes 8454148
